TPU v7x, 32 devices: a whole 2x2x4 slice. The times are simulated.
32 devices in a mesh: groups: 2 (over y), row: 8 (over z, x), col: 2 (over core).
Axes of the slice: x: 2, y: 2, z: 4, core: 2. Of those that a mesh axis runs over, the one named last changes fastest.
Arguments:
- queries: float32 [128, 4096], P(('groups', 'row'), 'col'), parts along dimension 0, may hold values from -3 to 3
- documents: float32 [128, 4096], P(('groups', 'row'), 'col'), parts along dimension 0, may hold values from -3 to 3
- positive: int32 [128], P(('groups', 'row')), parts along dimension 0, may hold values from 0 to 63, as said below
- hard_ids: int32 [128, 7], P(('groups', 'row')), parts along dimension 0, may hold values from 0 to 63
Outputs:
- request_derivative: float32 [128, 4096], P(('groups', 'row'), 'col'), parts along dimension 0
- passage_derivative: float32 [128, 4096], P(('groups', 'row'), 'col'), parts along dimension 0
- loss_rows: float32 [128], P(('groups', 'row')), parts along dimension 0
There are 2 independent parts, one for each index of `groups`. A program takes and returns all parts, laid end to end along the dimension named above; each array names one. Nothing has to cross between parts.
Inputs may be any that keep to these rules, and one draw needn't show every extreme that they name: positive[i] is a document of query i's own aligned block of 8, from i - i % 8 to i - i % 8 + 7; within each block every document is the positive of exactly one query.
All inputs are finite; a program needn't handle non-finite values.
Results may differ from a plain program's by a relative error of at most 0.006.
Values may be sent and summed in bfloat16 or wider, within the bound.
No kernel may reach another device: no remote copies, remote signals or barrier semaphores. Data moves between devices by JAX's collectives and lax.ppermute only.
A program may use at most 64 MiB of HBM per device.

v0:
```python
import jax
import jax.numpy as jnp
from jax import lax
from jax.sharding import PartitionSpec as P

sharpness_divisor = 0.05
hardness_multiplier = 3.0


def weigh(request_similarity, passage_similarity, positive, hard_ids, batch_size):
    columns = jnp.arange(batch_size, dtype=jnp.int32)
    hardness_tally = jnp.zeros(request_similarity.shape, jnp.float32)
    for column in range(hard_ids.shape[1]):
        hardness_tally = hardness_tally + (hard_ids[:, column][:, None] == columns[None, :]).astype(
            jnp.float32
        )
    request_raw_similarity = request_similarity / sharpness_divisor + jnp.log1p(
        hardness_multiplier * hardness_tally
    )
    matching_indicator = positive[:, None] == columns[None, :]
    passage_raw_similarity = jnp.where(
        matching_indicator, -jnp.inf, passage_similarity / sharpness_divisor
    )
    row_peak = jnp.maximum(
        jnp.max(request_raw_similarity, axis=1), jnp.max(passage_raw_similarity, axis=1)
    )
    row_mass = jnp.sum(jnp.exp(request_raw_similarity - row_peak[:, None]), axis=1) + jnp.sum(
        jnp.exp(passage_raw_similarity - row_peak[:, None]), axis=1
    )
    row_lse = row_peak + jnp.log(row_mass)
    loss_rows = row_lse - jnp.sum(
        jnp.where(matching_indicator, request_raw_similarity, 0.0), axis=1
    )
    request_probability = jnp.exp(request_raw_similarity - row_lse[:, None]).astype(jnp.bfloat16)
    passage_probability = jnp.exp(passage_raw_similarity - row_lse[:, None]).astype(jnp.bfloat16)
    return (request_probability, passage_probability, loss_rows)


def contract_first(left, right):
    return lax.dot_general(
        left, right, (((0,), (0,)), ((), ())), preferred_element_type=jnp.float32
    )


def on_device(queries, documents, positive, hard_ids):
    row_count = queries.shape[0]
    batch_size = row_count * lax.axis_size("row")
    offset = lax.axis_index("row") * row_count
    request_matrix = queries.astype(jnp.bfloat16)
    passage_matrix = documents.astype(jnp.bfloat16)
    local_pos = positive - offset
    picker = local_pos[:, None] == jnp.arange(row_count, dtype=jnp.int32)[None, :]
    reference_side_entries = jnp.take(passage_matrix, local_pos, axis=0)
    document_gathered, query_all = (
        lax.all_gather(passage_matrix, "row", axis=0, tiled=True),
        lax.all_gather(request_matrix, "row", axis=0, tiled=True),
    )
    stacked = jnp.concatenate([request_matrix, reference_side_entries], axis=0)
    partial_value = lax.dot_general(
        stacked, document_gathered, (((1,), (1,)), ((), ())), preferred_element_type=jnp.float32
    )
    query_part = partial_value[:row_count]
    doc_part = partial_value[row_count:]
    request_similarity, passage_similarity = lax.psum((query_part, doc_part), "col")
    request_probability, passage_probability, loss_rows = weigh(
        request_similarity, passage_similarity, positive, hard_ids, batch_size
    )
    request_derivative = (
        jnp.dot(request_probability, document_gathered, preferred_element_type=jnp.float32)
        - reference_side_entries.astype(jnp.float32)
    ) / sharpness_divisor
    reference_side_derivative = (
        jnp.dot(passage_probability, document_gathered, preferred_element_type=jnp.float32)
        / sharpness_divisor
    )
    forwarded_entries = (
        reference_side_derivative - request_matrix.astype(jnp.float32) / sharpness_divisor
    )
    permuted = contract_first(picker.astype(jnp.bfloat16), passage_probability).astype(jnp.bfloat16)
    query_columns, anchor_columns = (
        lax.all_to_all(request_probability, "row", split_axis=1, concat_axis=0, tiled=True),
        lax.all_to_all(permuted, "row", split_axis=1, concat_axis=0, tiled=True),
    )
    anchor_contribution = contract_first(anchor_columns, document_gathered)
    query_contribution = contract_first(query_columns, query_all)
    dispersion_level = lax.dot_general(
        picker.astype(jnp.float32),
        forwarded_entries,
        (((0,), (0,)), ((), ())),
        precision=lax.Precision.HIGHEST,
        preferred_element_type=jnp.float32,
    )
    passage_derivative = (
        query_contribution + anchor_contribution
    ) / sharpness_divisor + dispersion_level
    return (request_derivative, passage_derivative, loss_rows)


def solution(mesh):
    return jax.shard_map(
        on_device,
        mesh=mesh,
        in_specs=(
            P(("groups", "row"), "col"),
            P(("groups", "row"), "col"),
            P(("groups", "row")),
            P(("groups", "row"), None),
        ),
        out_specs=(P(("groups", "row"), "col"), P(("groups", "row"), "col"), P(("groups", "row"))),
        check_vma=False,
    )
```

profile of v0, /device:TPU:0, one launch (start us, length us, event | category | flops | bytes accessed | tf_op | source)
XLA Modules:
  0.0 89.3 jit_solution(14401006248320287965)
XLA Ops:
  0.6 0.6 copy-done.2
  1.3 0.8 convert_element_type.45
  2.2 32.5 %all_gather.6 = bf16[64,2048]{1,0:T(8,128)(2,1)S(1)} all-gather(bf16[8,2048]{1,0:T(8,128)(2,1)S(1)} %convert_element_type.45), channel_id=1, replica_groups=mesh['groups'=2,'row'=8,'col'=2] {'row'}, dimensions={0}, use_global_device_ids=true | all-gather | bytes 294912 | tf_op jit(solution)/shard_map/all_gather | solution.py:55
  34.7 0.6 gather_fusion
  35.3 0.3 copy-done.1
  35.6 0.2 fusion.3
  35.8 0.7 copy-done
  36.5 0.3 slice_reduce_fusion.6
  36.8 2.5 %all-reduce = (f32[8,64]{1,0:T(8,128)S(1)}, f32[8,64]{1,0:T(8,128)S(1)}) all-reduce(f32[8,64]{1,0:T(8,128)S(1)} %get-tuple-element.22, f32[8,64]{1,0:T(8,128)S(1)} %get-tuple-element.21), channel_id=1, replica_groups=mesh['groups'=2,'row'=8,'col'=2] {'col'}, use_global_device_ids=true, to_apply=%region_0.1 | all-reduce | flops 1024 | bytes 8192 | tf_op jit(solution)/shard_map/psum | solution.py:64
  39.3 0.2 fusion.12
  39.5 0.2 select_reduce_fusion
  39.7 0.5 fusion.11
  40.3 0.7 copy.13
  41.0 5.5 %all-to-all-start = ((bf16[8,8,8]{0,2,1:T(8,128)(2,1)}), bf16[8,8,8]{0,2,1:T(8,128)(2,1)S(1)}, u32[]{:S(2)}, u32[]{:S(2)}) async-start(bf16[8,8,8]{0,2,1:T(8,128)(2,1)} %bitcast), calls=%async_computation | async-start | bytes 32768 | tf_op jit(solution)/shard_map/all_to_all | solution.py:81
  46.5 0.8 fusion.2
  47.3 0.2 fusion
  47.5 0.3 convolution_convert_fusion
  47.7 0.7 copy.14
  48.4 4.7 %all-to-all-done = bf16[8,8,8]{0,2,1:T(8,128)(2,1)S(1)} async-done(((bf16[8,8,8]{0,2,1:T(8,128)(2,1)}), bf16[8,8,8]{0,2,1:T(8,128)(2,1)S(1)}, u32[]{:S(2)}, u32[]{:S(2)}) %all-to-all-start) | async-done | bytes 1056 | tf_op jit(solution)/shard_map/all_to_all | solution.py:81
  53.1 3.3 %all-to-all-start.1 = ((bf16[8,8,8]{0,2,1:T(8,128)(2,1)}), bf16[8,8,8]{0,2,1:T(8,128)(2,1)S(1)}, u32[]{:S(2)}, u32[]{:S(2)}) async-start(bf16[8,8,8]{0,2,1:T(8,128)(2,1)} %bitcast.2), calls=%async_computation.1 | async-start | bytes 32768 | tf_op jit(solution)/shard_map/all_to_all | solution.py:82
  56.4 31.4 %all_gather.7 = bf16[64,2048]{1,0:T(8,128)(2,1)S(1)} all-gather(bf16[8,2048]{1,0:T(8,128)(2,1)S(1)} %convert_element_type.44), channel_id=1, replica_groups=mesh['groups'=2,'row'=8,'col'=2] {'row'}, dimensions={0}, use_global_device_ids=true | all-gather | bytes 294912 | tf_op jit(solution)/shard_map/all_gather | solution.py:56
  88.1 0.1 fusion.14
  88.2 0.2 fusion.1
  88.4 0.9 %convolution_add_fusion = f32[8,2048]{1,0:T(8,128)} fusion(f32[8,2048]{1,0:T(8,128)S(1)} %fusion.1, f32[8,2048]{1,0:T(8,128)S(1)} %fusion, s32[8]{0:T(128)S(1)} %get-tuple-element.20), kind=kOutput, calls=%fused_computation.1 | convolution fusion | flops 1589312 | bytes 196640 | tf_op jit(solution)/shard_map/dot_general | solution.py:86
  (16 shorter events, 0.4 us)
Async XLA Ops:
  0.6 0.7 copy-start.2
  34.7 0.8 copy-start.1
  35.8 0.7 copy-start
  41.0 12.1 %all-to-all-start = ((bf16[8,8,8]{0,2,1:T(8,128)(2,1)}), bf16[8,8,8]{0,2,1:T(8,128)(2,1)S(1)}, u32[]{:S(2)}, u32[]{:S(2)}) async-start(bf16[8,8,8]{0,2,1:T(8,128)(2,1)} %bitcast), calls=%async_computation | async-start | bytes 32768 | tf_op jit(solution)/shard_map/all_to_all | solution.py:81
  53.1 34.9 %all-to-all-start.1 = ((bf16[8,8,8]{0,2,1:T(8,128)(2,1)}), bf16[8,8,8]{0,2,1:T(8,128)(2,1)S(1)}, u32[]{:S(2)}, u32[]{:S(2)}) async-start(bf16[8,8,8]{0,2,1:T(8,128)(2,1)} %bitcast.2), calls=%async_computation.1 | async-start | bytes 32768 | tf_op jit(solution)/shard_map/all_to_all | solution.py:82
where the time goes:
time: 89.7 us; the launch traced here: 89.3 us
  blocking collectives  66.5 us (74%)
  starting transfers between devices  8.86 us (10%)
  waiting for transfers between devices  4.7 us (5%)
  local copies, waits for them, and re-layouts  4.02 us (4%)
  matrix products  2.58 us (3%)
  other arithmetic  1.98 us (2%)
    all_gather x1, blocking collectives, on_device(): lax.all_gather(passage_matrix, 'row', axis=0, tiled=True)  32.5 us
    all_gather x1, blocking collectives, on_device(): lax.all_gather(request_matrix, 'row', axis=0, tiled=True)  31.4 us
    all_to_all x1, starting transfers between devices, on_device(): lax.all_to_all(request_probability, 'row', split_axis=1, concat_axis=0, t...  5.52 us
    all_to_all x1, waiting for transfers between devices, on_device(): lax.all_to_all(request_probability, 'row', split_axis=1, concat_axis=0, t...  4.7 us
    all_to_all x1, starting transfers between devices, on_device(): lax.all_to_all(permuted, 'row', split_axis=1, concat_axis=0, tiled=True)  3.33 us
    psum x1, blocking collectives, on_device(): lax.psum((query_part, doc_part), 'col')  2.5 us
  transfers between devices with their start and end apart: 2, of which 1 were waited for; matrix products, arithmetic and copies ran while one was open for 2% of the time, Pallas kernels for 0%

commit v1 on v0

--- a/solution.py
+++ b/solution.py
@@ -1,10 +1,200 @@
+import functools
+
 import jax
 import jax.numpy as jnp
 from jax import lax
+from jax.experimental import pallas as pl
+from jax.experimental.pallas import tpu as pltpu
 from jax.sharding import PartitionSpec as P
 
 sharpness_divisor = 0.05
 hardness_multiplier = 3.0
+LANES = 128
+VMEM = pl.BlockSpec(memory_space=pltpu.VMEM)
+SMEM = pl.BlockSpec(memory_space=pltpu.SMEM)
+HBM = pl.BlockSpec(memory_space=pltpu.HBM)
+PARAMS = pltpu.CompilerParams(vmem_limit_bytes=8 << 20)
+
+
+def slot_matrix(positive_ref, rows):
+    slots = lax.broadcasted_iota(jnp.int32, (rows, rows), 0)
+    places = lax.broadcasted_iota(jnp.int32, (rows, rows), 1)
+    hit = jnp.zeros((rows, rows), jnp.float32)
+    for i in range(rows):
+        local = lax.rem(positive_ref[i], rows)
+        hit = jnp.where((places == i) & (slots == local), 1.0, hit)
+    return hit
+
+
+def pack_kernel(
+    positive_hbm, query_hbm, doc_hbm, hard_hbm, out_ref, positive_ref, query_ref, doc_ref, hard_ref, sems
+):
+    copies = [
+        pltpu.make_async_copy(source, target, sems.at[n])
+        for n, (source, target) in enumerate(
+            (
+                (positive_hbm, positive_ref),
+                (query_hbm, query_ref),
+                (doc_hbm, doc_ref),
+                (hard_hbm, hard_ref),
+            )
+        )
+    ]
+    for copy in copies:
+        copy.start()
+    for copy in copies:
+        copy.wait()
+    rows, width = query_ref.shape
+    tail = out_ref.shape[1] - width
+    hit = slot_matrix(positive_ref, rows)
+    queries = jnp.dot(
+        hit.astype(jnp.bfloat16),
+        query_ref[...].astype(jnp.bfloat16),
+        preferred_element_type=jnp.float32,
+    )
+    lane = lax.broadcasted_iota(jnp.int32, (rows, tail), 1)
+    block, place = lane // (2 * rows), lax.rem(lane, 2 * rows)
+    column = jnp.where(place >= rows, block * rows + place - rows, -1)
+    hard = hard_ref[...]
+    counts = jnp.zeros((rows, tail), jnp.float32)
+    for k in range(hard.shape[1]):
+        counts = counts + jnp.where(hard[:, k][:, None] == column, 1.0, 0.0)
+    counts = jnp.dot(
+        hit.astype(jnp.bfloat16), counts.astype(jnp.bfloat16), preferred_element_type=jnp.float32
+    )
+    upper = jnp.concatenate([queries, counts], axis=1)
+    lower = jnp.concatenate([doc_ref[...], jnp.zeros((rows, tail), jnp.float32)], axis=1)
+    out_ref[...] = jnp.concatenate([upper, lower], axis=0).astype(jnp.bfloat16)
+
+
+def score_kernel(masks, width, *refs):
+    *block_refs, all_ref, score_ref = refs
+    me = lax.axis_index("row")
+    side = lax.axis_index("col")
+    for ref, (first, second) in zip(block_refs, masks):
+        for n, (a, b) in enumerate(zip(first, second)):
+            mask = a if a == b else jnp.where(side == 0, a, b)
+            value = ref[...] if len(ref.shape) == 2 else ref[n]
+            all_ref[lax.bitwise_xor(me, mask)] = value
+    blocks, height, depth = all_ref.shape
+    rows = all_ref[...].reshape(blocks * height, depth)[:, :width]
+    score_ref[...] = lax.dot_general(
+        rows, rows, (((1,), (1,)), ((), ())), preferred_element_type=jnp.float32
+    )
+
+
+def finish_kernel(
+    width, positive_ref, own_ref, other_ref, all_ref, request_ref, passage_ref, loss_ref, hold
+):
+    me = lax.axis_index("row")
+    blocks, height, depth = all_ref.shape
+    rows, total = height // 2, blocks * height
+    scores = (own_ref[...] + other_ref[...]) / sharpness_divisor
+    counts = all_ref[...].reshape(total, depth)[:, width:].astype(jnp.float32)
+    row = lax.broadcasted_iota(jnp.int32, (total, total), 0)
+    lane = lax.broadcasted_iota(jnp.int32, (total, total), 1)
+    is_document = lax.rem(lane, height) >= rows
+    logits = jnp.where(
+        is_document & (row != lane), scores + jnp.log1p(hardness_multiplier * counts), -jnp.inf
+    ).reshape(blocks, 2, rows, total)
+    peak = jnp.max(jnp.max(logits, axis=1), axis=-1, keepdims=True)
+    mass = jnp.sum(jnp.sum(jnp.exp(logits - peak[:, None]), axis=1), axis=-1, keepdims=True)
+    lse = peak + jnp.log(mass)
+    weights = jnp.exp(logits - lse[:, None]).reshape(total, total)
+    hold[0] = weights.reshape(blocks, height, total)
+    hold[1] = weights.T.reshape(blocks, height, total)
+    hold[2] = logits.reshape(blocks, height, total)
+    hit = slot_matrix(positive_ref, rows)
+    back = hit.T.astype(jnp.bfloat16)
+    mine = hold[0, me].astype(jnp.bfloat16)
+    onto = hold[1, me].astype(jnp.bfloat16)
+    request_weights = jnp.dot(back, mine[:rows], preferred_element_type=jnp.float32).astype(jnp.bfloat16)
+    left = jnp.concatenate([request_weights, mine[rows:], onto], axis=0)
+    values = all_ref[...].reshape(total, depth)[:, :width]
+    product = jnp.dot(left, values, preferred_element_type=jnp.float32)
+    block = all_ref[me]
+    anchors = jnp.dot(back, block[rows:, :width], preferred_element_type=jnp.float32)
+    request_ref[...] = (product[:rows] - anchors) / sharpness_divisor
+    passage_ref[...] = (
+        product[rows : 2 * rows] + product[3 * rows :] - block[:rows, :width].astype(jnp.float32)
+    ) / sharpness_divisor
+    own_logits = hold[2, me][:rows]
+    slot = lax.broadcasted_iota(jnp.int32, (rows, total), 0) + me * height + rows
+    at = lax.broadcasted_iota(jnp.int32, (rows, total), 1)
+    picked = jnp.sum(jnp.where(slot == at, own_logits, 0.0), axis=1, keepdims=True)
+    again = jnp.max(hold[2, me].reshape(2, rows, total), axis=0)
+    top = jnp.max(again, axis=1, keepdims=True)
+    spread = jnp.exp(hold[2, me].reshape(2, rows, total) - top[None])
+    own_lse = top + jnp.log(jnp.sum(jnp.sum(spread, axis=0), axis=1, keepdims=True))
+    loss_ref[...] = jnp.sum(hit * (own_lse - picked), axis=0)
+
+
+def exchange(value, masks):
+    count = lax.axis_size("row")
+    sides = lax.axis_size("col")
+    pairs = [
+        (sides * i + c, sides * (i ^ masks[c]) + c) for i in range(count) for c in range(sides)
+    ]
+    return lax.ppermute(value, ("row", "col"), pairs)
+
+
+PLAN = (((0,), (1, 4)), ((0, 1), (4, 2)), ((0, 1, 2), (2, 1)))
+
+
+def on_device_fast(queries, documents, positive, hard_ids):
+    rows, width = queries.shape
+    count = lax.axis_size("row")
+    height, total = 2 * rows, 2 * rows * count
+    tail = -(-total // LANES) * LANES
+    block = pl.pallas_call(
+        pack_kernel,
+        out_shape=jax.ShapeDtypeStruct((height, width + tail), jnp.bfloat16),
+        in_specs=[HBM, HBM, HBM, HBM],
+        out_specs=VMEM,
+        scratch_shapes=[
+            pltpu.SMEM(positive.shape, positive.dtype),
+            pltpu.VMEM(queries.shape, queries.dtype),
+            pltpu.VMEM(documents.shape, documents.dtype),
+            pltpu.VMEM(hard_ids.shape, hard_ids.dtype),
+            pltpu.SemaphoreType.DMA((4,)),
+        ],
+        compiler_params=PARAMS,
+        name="pack",
+    )(positive, queries, documents, hard_ids)
+    pieces, masks = [block[None]], [([0], [0])]
+    for step, (sources, hops) in enumerate(PLAN):
+        with jax.named_scope(f"hop{step}"):
+            held = [pieces[n] for n in sources]
+            held = held[0] if len(held) == 1 else jnp.concatenate(held, axis=0)
+            pieces.append(exchange(held, hops))
+        masks.append(
+            tuple([m ^ hops[c] for n in sources for m in masks[n][c]] for c in range(len(hops)))
+        )
+    everything, own = pl.pallas_call(
+        functools.partial(score_kernel, masks, width),
+        out_shape=(
+            jax.ShapeDtypeStruct((count, height, width + tail), jnp.bfloat16),
+            jax.ShapeDtypeStruct((total, total), jnp.float32),
+        ),
+        in_specs=[VMEM] * len(pieces),
+        out_specs=(VMEM, VMEM),
+        compiler_params=PARAMS,
+        name="score",
+    )(*pieces)
+    other = lax.ppermute(own, "col", [(0, 1), (1, 0)])
+    return pl.pallas_call(
+        functools.partial(finish_kernel, width),
+        out_shape=(
+            jax.ShapeDtypeStruct((rows, width), jnp.float32),
+            jax.ShapeDtypeStruct((rows, width), jnp.float32),
+            jax.ShapeDtypeStruct((rows,), jnp.float32),
+        ),
+        in_specs=[SMEM, VMEM, VMEM, VMEM],
+        out_specs=(VMEM, VMEM, VMEM),
+        scratch_shapes=[pltpu.VMEM((3, count, height, total), jnp.float32)],
+        compiler_params=PARAMS,
+        name="finish",
+    )(positive, own, other, everything)
 
 
 def weigh(request_similarity, passage_similarity, positive, hard_ids, batch_size):
@@ -42,7 +232,7 @@
     )
 
 
-def on_device(queries, documents, positive, hard_ids):
+def on_device_wide(queries, documents, positive, hard_ids):
     row_count = queries.shape[0]
     batch_size = row_count * lax.axis_size("row")
     offset = lax.axis_index("row") * row_count
@@ -97,8 +287,9 @@
 
 
 def solution(mesh):
+    small = mesh.shape["row"] == 8 and mesh.shape["col"] == 2
     return jax.shard_map(
-        on_device,
+        on_device_fast if small else on_device_wide,
         mesh=mesh,
         in_specs=(
             P(("groups", "row"), "col"),

time: 89.7 us -> 27 us (0.30)
  blocking collectives: 66.5 us -> 0 us
  waiting for transfers between devices: 4.7 us -> 11.2 us
  Pallas kernels: 0 us -> 2.92 us
  matrix products: 2.58 us -> 0 us
  other arithmetic: 1.98 us -> 0.05 us
  local copies, waits for them, and re-layouts: 4.02 us -> 3.02 us
    all_gather x2 -> x0, blocking collectives: 64 us -> none  [the longest x1 32.5 us: on_device(): lax.all_gather(passage_matrix, 'row', axis=0, tiled=True)]
    ppermute x0 -> x4, waiting for transfers between devices: none -> 11.2 us  [the longest x3 9.99 us: exchange(): return lax.ppermute(value, ('row', 'col'), pairs)]
    all_to_all x2 -> x0, starting transfers between devices: 8.86 us -> none  [the longest x1 5.52 us: on_device(): lax.all_to_all(request_probability, 'row', split_axis=1, concat_axis=0, t...]
    ppermute x0 -> x4, starting transfers between devices: none -> 8.8 us  [the longest x3 8.73 us: exchange(): return lax.ppermute(value, ('row', 'col'), pairs)]
    all_to_all x2 -> x0, waiting for transfers between devices: 4.7 us -> none  [the longest x1 4.7 us: on_device(): lax.all_to_all(request_probability, 'row', split_axis=1, concat_axis=0, t...]
    pallas_call x0 -> x3, Pallas kernels: none -> 2.92 us  [the longest x1 1.8 us: on_device_fast(): pl.pallas_call(functools.partial(finish_kernel, width), out_shape=(jax.Sh...]
    dot_general x7 -> x0, matrix products: 2.58 us -> none  [the longest x1 0.92 us: on_device(): lax.dot_general(picker.astype(jnp.float32), forwarded_entries, (((0,), (0...]
    psum x1 -> x0, blocking collectives: 2.5 us -> none  [on_device(): lax.psum((query_part, doc_part), 'col')]
  transfers between devices with their start and end apart: 2 -> 4, of which waited for: 1 -> 4; matrix products, arithmetic and copies ran while one was open for 2% -> 0% of each run, Pallas kernels for 0% -> 0%
where the time goes in v1:
time: 27 us; the launch traced here: 26.7 us
  waiting for transfers between devices  11.2 us (41%)
  starting transfers between devices  8.8 us (33%)
  local copies, waits for them, and re-layouts  3.02 us (11%)
  Pallas kernels  2.92 us (11%)
  between operations  0.68 us (3%)
    ppermute x3, waiting for transfers between devices, exchange(): return lax.ppermute(value, ('row', 'col'), pairs)  9.99 us
    ppermute x3, starting transfers between devices, exchange(): return lax.ppermute(value, ('row', 'col'), pairs)  8.73 us
    unnamed x10, local copies, waits for them, and re-layouts  3.02 us
    pallas_call x1, Pallas kernels, on_device_fast(): pl.pallas_call(functools.partial(finish_kernel, width), out_shape=(jax.Sh...  1.8 us
    ppermute x1, waiting for transfers between devices, on_device_fast(): other = lax.ppermute(own, 'col', [(0, 1), (1, 0)])  1.24 us
    pallas_call x1, Pallas kernels, on_device_fast(): pl.pallas_call(pack_kernel, out_shape=jax.ShapeDtypeStruct((height, width...  0.78 us
  transfers between devices with their start and end apart: 4, of which 4 were waited for; matrix products, arithmetic and copies ran while one was open for 0% of the time, Pallas kernels for 0%

profile of v1, /device:TPU:0, one launch (start us, length us, event | category | flops | bytes accessed | tf_op | source)
XLA Modules:
  0.0 26.7 jit_solution(8165312005185551013)
XLA Ops:
  0.6 0.0 copy-start
  0.6 0.8 %copy-done = f32[8,2048]{1,0:T(8,128)S(1)} copy-done((f32[8,2048]{1,0:T(8,128)S(1)}, f32[8,2048]{1,0:T(8,128)}, u32[]{:S(2)}) %copy-start) | copy-done | bytes 65560
  1.5 0.0 copy-start.1
  1.5 0.8 %copy-done.1 = f32[8,2048]{1,0:T(8,128)S(1)} copy-done((f32[8,2048]{1,0:T(8,128)S(1)}, f32[8,2048]{1,0:T(8,128)}, u32[]{:S(2)}) %copy-start.1) | copy-done | bytes 65560
  2.3 0.0 copy-start.2
  2.3 0.7 %copy-done.2 = s32[8,7]{1,0:T(8,128)S(1)} copy-done((s32[8,7]{1,0:T(8,128)S(1)}, s32[8,7]{1,0:T(8,128)}, u32[]{:S(2)}) %copy-start.2) | copy-done | bytes 248
  3.0 0.0 copy-start.3
  3.0 0.7 %copy-done.3 = s32[8]{0:T(128)S(1)} copy-done((s32[8]{0:T(128)S(1)}, s32[8]{0:T(128)}, u32[]{:S(2)}) %copy-start.3) | copy-done | bytes 56
  3.7 0.8 %pack.1 = bf16[16,2176]{1,0:T(8,128)(2,1)S(1)} custom-call(s32[8]{0:T(128)S(1)} %copy-done.3, f32[8,2048]{1,0:T(8,128)S(1)} %copy-done, f32[8,2048]{1,0:T(8,128)S(1)} %copy-done.1, s32[8,7]{1,0:T(8,128)S(1)} %copy-done.2), custom_call_target="tpu_custom_call" | custom-call | tf_op jit(solution)/shard_map/pack/pallas_call | solution.py:149
  4.4 3.0 %collective-permute-start = (bf16[1,16,2176]{2,1,0:T(8,128)(2,1)S(1)}, bf16[1,16,2176]{2,1,0:T(8,128)(2,1)S(1)}, u32[]{:S(2)}, u32[]{:S(2)}) collective-permute-start(bf16[1,16,2176]{2,1,0:T(8,128)(2,1)S(1)} %bitcast.1), channel_id=1, source_target_pairs={{0,2},{1,9},{2,0},{3,11},{4,6},{5,13},{6,4},{7,15},{8,10},{9,1},{1... | collective-permute-start | bytes 208904 | tf_op jit(solution)/shard_map/hop0/ppermute | solution.py:138
  7.5 2.3 %collective-permute-done.refs_1_ = bf16[1,16,2176]{2,1,0:T(8,128)(2,1)S(1)} collective-permute-done((bf16[1,16,2176]{2,1,0:T(8,128)(2,1)S(1)}, bf16[1,16,2176]{2,1,0:T(8,128)(2,1)S(1)}, u32[]{:S(2)}, u32[]{:S(2)}) %collective-permute-start) | collective-permute-done | bytes 69664 | tf_op jit(solution)/shard_map/hop0/ppermute | solution.py:138
  9.8 3.2 %collective-permute-start.1 = (bf16[2,16,2176]{2,1,0:T(8,128)(2,1)S(1)}, bf16[2,16,2176]{2,1,0:T(8,128)(2,1)S(1)}, u32[]{:S(2)}, u32[]{:S(2)}) collective-permute-start(bf16[2,16,2176]{2,1,0:T(8,128)(2,1)S(1)} %pad_maximum_fusion.1), channel_id=1, source_target_pairs={{0,8},{1,5},{2,10},{3,7},{4,12},{5,1},{6,14},{7,3},{8,0},{9,13},{1... | collective-permute-start | bytes 417800 | tf_op jit(solution)/shard_map/hop1/ppermute | solution.py:138
  13.0 3.2 %collective-permute-done.1.refs_2_ = bf16[2,16,2176]{2,1,0:T(8,128)(2,1)S(1)} collective-permute-done((bf16[2,16,2176]{2,1,0:T(8,128)(2,1)S(1)}, bf16[2,16,2176]{2,1,0:T(8,128)(2,1)S(1)}, u32[]{:S(2)}, u32[]{:S(2)}) %collective-permute-start.1) | collective-permute-done | bytes 139296 | tf_op jit(solution)/shard_map/hop1/ppermute | solution.py:138
  16.2 2.5 %collective-permute-start.2 = (bf16[4,16,2176]{2,1,0:T(8,128)(2,1)S(1)}, bf16[4,16,2176]{2,1,0:T(8,128)(2,1)S(1)}, u32[]{:S(2)}, u32[]{:S(2)}) collective-permute-start(bf16[4,16,2176]{2,1,0:T(8,128)(2,1)S(1)} %pad_maximum_fusion), channel_id=1, source_target_pairs={{0,4},{1,3},{2,6},{3,1},{4,0},{5,7},{6,2},{7,5},{8,12},{9,11},{10,... | collective-permute-start | bytes 835592 | tf_op jit(solution)/shard_map/hop2/ppermute | solution.py:138
  18.7 4.5 %collective-permute-done.2.refs_3_ = bf16[4,16,2176]{2,1,0:T(8,128)(2,1)S(1)} collective-permute-done((bf16[4,16,2176]{2,1,0:T(8,128)(2,1)S(1)}, bf16[4,16,2176]{2,1,0:T(8,128)(2,1)S(1)}, u32[]{:S(2)}, u32[]{:S(2)}) %collective-permute-start.2) | collective-permute-done | bytes 278560 | tf_op jit(solution)/shard_map/hop2/ppermute | solution.py:138
  23.2 0.3 %score.1 = (bf16[8,16,2176]{2,1,0:T(8,128)(2,1)S(1)}, f32[128,128]{1,0:T(8,128)S(1)}) custom-call(bf16[1,16,2176]{2,1,0:T(8,128)(2,1)S(1)} %bitcast.4, bf16[1,16,2176]{2,1,0:T(8,128)(2,1)S(1)} %collective-permute-done.refs_1_, bf16[2,16,2176]{2,1,0:T(8,128)(2,1)S(1)} %collective-permute-done.1.refs_2_, bf16[4,16,2176]{2,1,0:T(8,128)(2,1)S(1)} %collective-permute-done.2.refs_3_), custom_call_target="tpu_custom_call" | custom-call | tf_op jit(solution)/shard_map/score/pallas_call | solution.py:173
  23.6 0.0 copy-start.4
  23.6 0.1 collective-permute-start.3
  23.7 1.2 %collective-permute-done.3.other_ref = f32[128,128]{1,0:T(8,128)S(1)} collective-permute-done((f32[128,128]{1,0:T(8,128)S(1)}, f32[128,128]{1,0:T(8,128)S(1)}, u32[]{:S(2)}, u32[]{:S(2)}) %collective-permute-start.3) | collective-permute-done | bytes 65568 | tf_op jit(solution)/shard_map/ppermute | solution.py:184
  24.9 0.0 copy-done.4
  24.9 1.8 %finish.1 = (f32[8,2048]{1,0:T(8,128)}, f32[8,2048]{1,0:T(8,128)}, f32[8]{0:T(128)}) custom-call(s32[8]{0:T(128)S(1)} %copy-done.4, f32[128,128]{1,0:T(8,128)S(1)} %get-tuple-element.5.own_ref, f32[128,128]{1,0:T(8,128)S(1)} %collective-permute-done.3.other_ref, bf16[8,16,2176]{2,1,0:T(8,128)(2,1)S(1)} %get-tuple-element.6.all_ref), custom_call_target="tpu_custom_call" | custom-call | tf_op jit(solution)/shard_map/finish/pallas_call | solution.py:185
  (2 shorter events, 0.1 us)
Async XLA Ops:
  0.6 0.8 %copy-start = (f32[8,2048]{1,0:T(8,128)S(1)}, f32[8,2048]{1,0:T(8,128)}, u32[]{:S(2)}) copy-start(f32[8,2048]{1,0:T(8,128)} %query_hbm.1) | copy-start | bytes 196612
  1.5 0.8 %copy-start.1 = (f32[8,2048]{1,0:T(8,128)S(1)}, f32[8,2048]{1,0:T(8,128)}, u32[]{:S(2)}) copy-start(f32[8,2048]{1,0:T(8,128)} %doc_hbm.1) | copy-start | bytes 196612
  2.3 0.7 %copy-start.2 = (s32[8,7]{1,0:T(8,128)S(1)}, s32[8,7]{1,0:T(8,128)}, u32[]{:S(2)}) copy-start(s32[8,7]{1,0:T(8,128)} %hard_hbm.1) | copy-start | bytes 676
  3.0 0.7 %copy-start.3 = (s32[8]{0:T(128)S(1)}, s32[8]{0:T(128)}, u32[]{:S(2)}) copy-start(s32[8]{0:T(128)} %positive_ref.1) | copy-start | bytes 100
  4.4 5.3 %collective-permute-start = (bf16[1,16,2176]{2,1,0:T(8,128)(2,1)S(1)}, bf16[1,16,2176]{2,1,0:T(8,128)(2,1)S(1)}, u32[]{:S(2)}, u32[]{:S(2)}) collective-permute-start(bf16[1,16,2176]{2,1,0:T(8,128)(2,1)S(1)} %bitcast.1), channel_id=1, source_target_pairs={{0,2},{1,9},{2,0},{3,11},{4,6},{5,13},{6,4},{7,15},{8,10},{9,1},{1... | collective-permute-start | bytes 208904 | tf_op jit(solution)/shard_map/hop0/ppermute | solution.py:138
  9.8 6.4 %collective-permute-start.1 = (bf16[2,16,2176]{2,1,0:T(8,128)(2,1)S(1)}, bf16[2,16,2176]{2,1,0:T(8,128)(2,1)S(1)}, u32[]{:S(2)}, u32[]{:S(2)}) collective-permute-start(bf16[2,16,2176]{2,1,0:T(8,128)(2,1)S(1)} %pad_maximum_fusion.1), channel_id=1, source_target_pairs={{0,8},{1,5},{2,10},{3,7},{4,12},{5,1},{6,14},{7,3},{8,0},{9,13},{1... | collective-permute-start | bytes 417800 | tf_op jit(solution)/shard_map/hop1/ppermute | solution.py:138
  16.2 7.0 %collective-permute-start.2 = (bf16[4,16,2176]{2,1,0:T(8,128)(2,1)S(1)}, bf16[4,16,2176]{2,1,0:T(8,128)(2,1)S(1)}, u32[]{:S(2)}, u32[]{:S(2)}) collective-permute-start(bf16[4,16,2176]{2,1,0:T(8,128)(2,1)S(1)} %pad_maximum_fusion), channel_id=1, source_target_pairs={{0,4},{1,3},{2,6},{3,1},{4,0},{5,7},{6,2},{7,5},{8,12},{9,11},{10,... | collective-permute-start | bytes 835592 | tf_op jit(solution)/shard_map/hop2/ppermute | solution.py:138
  23.6 1.3 %copy-start.4 = (s32[8]{0:T(128)S(1)}, s32[8]{0:T(128)}, u32[]{:S(2)}) copy-start(s32[8]{0:T(128)} %positive_ref.1) | copy-start | bytes 100
  23.6 1.3 %collective-permute-start.3 = (f32[128,128]{1,0:T(8,128)S(1)}, f32[128,128]{1,0:T(8,128)S(1)}, u32[]{:S(2)}, u32[]{:S(2)}) collective-permute-start(f32[128,128]{1,0:T(8,128)S(1)} %get-tuple-element.5.own_ref), channel_id=1, source_target_pairs={{0,1},{1,0},{2,3},{3,2},{4,5},{5,4},{6,7},{7,6},{8,9},{9,8},{10,11... | collective-permute-start | bytes 196616 | tf_op jit(solution)/shard_map/ppermute | solution.py:184

commit v2 on v1

--- a/solution.py
+++ b/solution.py
@@ -6,6 +6,7 @@
 from jax.experimental import pallas as pl
 from jax.experimental.pallas import tpu as pltpu
 from jax.sharding import PartitionSpec as P
+
 
 sharpness_divisor = 0.05
 hardness_multiplier = 3.0
@@ -138,7 +139,7 @@
     return lax.ppermute(value, ("row", "col"), pairs)
 
 
-PLAN = (((0,), (1, 4)), ((0, 1), (4, 2)), ((0, 1, 2), (2, 1)))
+PLAN = [((0,), (4, 4)), ((0,), (2, 2)), ((0,), (1, 1)), ((0, 1), (3, 3)), ((1,), (1, 1)), ((1,), (2, 2))]
 
 
 def on_device_fast(queries, documents, positive, hard_ids):
@@ -160,13 +161,12 @@
         ],
         compiler_params=PARAMS,
         name="pack",
-    )(positive, queries, documents, hard_ids)
+    )(*(pltpu.with_memory_space_constraint(v, pltpu.HBM) for v in (positive, queries, documents, hard_ids)))
     pieces, masks = [block[None]], [([0], [0])]
-    for step, (sources, hops) in enumerate(PLAN):
-        with jax.named_scope(f"hop{step}"):
-            held = [pieces[n] for n in sources]
-            held = held[0] if len(held) == 1 else jnp.concatenate(held, axis=0)
-            pieces.append(exchange(held, hops))
+    for sources, hops in PLAN:
+        held = [pieces[n] for n in sources]
+        held = held[0] if len(held) == 1 else jnp.concatenate(held, axis=0)
+        pieces.append(exchange(held, hops))
         masks.append(
             tuple([m ^ hops[c] for n in sources for m in masks[n][c]] for c in range(len(hops)))
         )

time: 27 us -> 21.8 us (0.81)
  waiting for transfers between devices: 11.2 us -> 7.86 us
  local copies, waits for them, and re-layouts: 3.02 us -> 0.01 us
  starting transfers between devices: 8.8 us -> 9.86 us
  Pallas kernels: 2.92 us -> 3.25 us
    ppermute x3 -> x6, waiting for transfers between devices: 9.99 us -> 6.62 us  [exchange(): return lax.ppermute(value, ('row', 'col'), pairs)]
    unnamed x10 -> x2, local copies, waits for them, and re-layouts: 3.02 us -> 0.01 us
    ppermute x3 -> x6, starting transfers between devices: 8.73 us -> 9.79 us  [exchange(): return lax.ppermute(value, ('row', 'col'), pairs)]
    pallas_call x1, Pallas kernels: 0.78 us -> 1.11 us  [on_device_fast(): pl.pallas_call(pack_kernel, out_shape=jax.ShapeDtypeStruct((height, width...]
  transfers between devices with their start and end apart: 4 -> 7, of which waited for: 4 -> 5; matrix products, arithmetic and copies ran while one was open for 0% -> 0% of each run, Pallas kernels for 0% -> 0%
where the time goes in v2:
time: 21.8 us; the launch traced here: 21.7 us
  starting transfers between devices  9.86 us (45%)
  waiting for transfers between devices  7.86 us (36%)
  Pallas kernels  3.25 us (15%)
  between operations  0.67 us (3%)
    ppermute x6, starting transfers between devices, exchange(): return lax.ppermute(value, ('row', 'col'), pairs)  9.79 us
    ppermute x6, waiting for transfers between devices, exchange(): return lax.ppermute(value, ('row', 'col'), pairs)  6.62 us
    pallas_call x1, Pallas kernels, on_device_fast(): pl.pallas_call(functools.partial(finish_kernel, width), out_shape=(jax.Sh...  1.8 us
    ppermute x1, waiting for transfers between devices, on_device_fast(): other = lax.ppermute(own, 'col', [(0, 1), (1, 0)])  1.24 us
    pallas_call x1, Pallas kernels, on_device_fast(): pl.pallas_call(pack_kernel, out_shape=jax.ShapeDtypeStruct((height, width...  1.11 us
  transfers between devices with their start and end apart: 7, of which 5 were waited for; matrix products, arithmetic and copies ran while one was open for 0% of the time, Pallas kernels for 0%

profile of v2, /device:TPU:0, one launch (start us, length us, event | category | flops | bytes accessed | tf_op | source)
XLA Modules:
  0.0 21.7 jit_solution(7076755788483975646)
XLA Ops:
  0.6 1.1 %pack.1 = bf16[16,2176]{1,0:T(8,128)(2,1)S(1)} custom-call(s32[8]{0:T(128)} %positive_ref.1, f32[8,2048]{1,0:T(8,128)} %query_hbm.1, f32[8,2048]{1,0:T(8,128)} %doc_hbm.1, s32[8,7]{1,0:T(8,128)} %hard_hbm.1), custom_call_target="tpu_custom_call" | custom-call | tf_op jit(solution)/shard_map/pack/pallas_call | solution.py:150
  1.7 4.1 %collective-permute-start = (bf16[1,16,2176]{2,1,0:T(8,128)(2,1)S(1)}, bf16[1,16,2176]{2,1,0:T(8,128)(2,1)S(1)}, u32[]{:S(2)}, u32[]{:S(2)}) collective-permute-start(bf16[1,16,2176]{2,1,0:T(8,128)(2,1)S(1)} %bitcast.1), channel_id=1, source_target_pairs={{0,8},{1,9},{2,10},{3,11},{4,12},{5,13},{6,14},{7,15},{8,0},{9,1},... | collective-permute-start | bytes 208904 | tf_op jit(solution)/shard_map/ppermute | solution.py:139
  5.9 3.8 %collective-permute-done.refs_1_ = bf16[1,16,2176]{2,1,0:T(8,128)(2,1)S(1)} collective-permute-done((bf16[1,16,2176]{2,1,0:T(8,128)(2,1)S(1)}, bf16[1,16,2176]{2,1,0:T(8,128)(2,1)S(1)}, u32[]{:S(2)}, u32[]{:S(2)}) %collective-permute-start) | collective-permute-done | bytes 69664 | tf_op jit(solution)/shard_map/ppermute | solution.py:139
  9.7 1.6 %collective-permute-start.3 = (bf16[2,16,2176]{2,1,0:T(8,128)(2,1)S(1)}, bf16[2,16,2176]{2,1,0:T(8,128)(2,1)S(1)}, u32[]{:S(2)}, u32[]{:S(2)}) collective-permute-start(bf16[2,16,2176]{2,1,0:T(8,128)(2,1)S(1)} %pad_maximum_fusion), channel_id=1, source_target_pairs={{0,6},{1,7},{2,4},{3,5},{4,2},{5,3},{6,0},{7,1},{8,14},{9,15},{10,... | collective-permute-start | bytes 417800 | tf_op jit(solution)/shard_map/ppermute | solution.py:139
  11.3 0.5 %collective-permute-start.2 = (bf16[1,16,2176]{2,1,0:T(8,128)(2,1)S(1)}, bf16[1,16,2176]{2,1,0:T(8,128)(2,1)S(1)}, u32[]{:S(2)}, u32[]{:S(2)}) collective-permute-start(bf16[1,16,2176]{2,1,0:T(8,128)(2,1)S(1)} %bitcast.3), channel_id=1, source_target_pairs={{0,2},{1,3},{2,0},{3,1},{4,6},{5,7},{6,4},{7,5},{8,10},{9,11},{10,... | collective-permute-start | bytes 208904 | tf_op jit(solution)/shard_map/ppermute | solution.py:139
  11.8 1.4 %collective-permute-start.1 = (bf16[1,16,2176]{2,1,0:T(8,128)(2,1)S(1)}, bf16[1,16,2176]{2,1,0:T(8,128)(2,1)S(1)}, u32[]{:S(2)}, u32[]{:S(2)}) collective-permute-start(bf16[1,16,2176]{2,1,0:T(8,128)(2,1)S(1)} %bitcast.4), channel_id=1, source_target_pairs={{0,4},{1,5},{2,6},{3,7},{4,0},{5,1},{6,2},{7,3},{8,12},{9,13},{10,... | collective-permute-start | bytes 208904 | tf_op jit(solution)/shard_map/ppermute | solution.py:139
  13.2 0.6 %collective-permute-start.5 = (bf16[1,16,2176]{2,1,0:T(8,128)(2,1)S(1)}, bf16[1,16,2176]{2,1,0:T(8,128)(2,1)S(1)}, u32[]{:S(2)}, u32[]{:S(2)}) collective-permute-start(bf16[1,16,2176]{2,1,0:T(8,128)(2,1)S(1)} %collective-permute-done.refs_1_), channel_id=1, source_target_pairs={{0,4},{1,5},{2,6},{3,7},{4,0},{5,1},{6,2},{7,3},{8,12},{9,13},{10,... | collective-permute-start | bytes 208904 | tf_op jit(solution)/shard_map/ppermute | solution.py:139
  13.8 1.5 %collective-permute-start.4 = (bf16[1,16,2176]{2,1,0:T(8,128)(2,1)S(1)}, bf16[1,16,2176]{2,1,0:T(8,128)(2,1)S(1)}, u32[]{:S(2)}, u32[]{:S(2)}) collective-permute-start(bf16[1,16,2176]{2,1,0:T(8,128)(2,1)S(1)} %collective-permute-done.refs_1_), channel_id=1, source_target_pairs={{0,2},{1,3},{2,0},{3,1},{4,6},{5,7},{6,4},{7,5},{8,10},{9,11},{10,... | collective-permute-start | bytes 208904 | tf_op jit(solution)/shard_map/ppermute | solution.py:139
  15.3 2.1 %collective-permute-done.2.refs_3_ = bf16[1,16,2176]{2,1,0:T(8,128)(2,1)S(1)} collective-permute-done((bf16[1,16,2176]{2,1,0:T(8,128)(2,1)S(1)}, bf16[1,16,2176]{2,1,0:T(8,128)(2,1)S(1)}, u32[]{:S(2)}, u32[]{:S(2)}) %collective-permute-start.2) | collective-permute-done | bytes 69664 | tf_op jit(solution)/shard_map/ppermute | solution.py:139
  17.4 0.0 collective-permute-done.1.refs_2_
  17.4 0.6 %collective-permute-done.5.refs_6_ = bf16[1,16,2176]{2,1,0:T(8,128)(2,1)S(1)} collective-permute-done((bf16[1,16,2176]{2,1,0:T(8,128)(2,1)S(1)}, bf16[1,16,2176]{2,1,0:T(8,128)(2,1)S(1)}, u32[]{:S(2)}, u32[]{:S(2)}) %collective-permute-start.5) | collective-permute-done | bytes 69664 | tf_op jit(solution)/shard_map/ppermute | solution.py:139
  18.0 0.2 %collective-permute-done.4.refs_5_ = bf16[1,16,2176]{2,1,0:T(8,128)(2,1)S(1)} collective-permute-done((bf16[1,16,2176]{2,1,0:T(8,128)(2,1)S(1)}, bf16[1,16,2176]{2,1,0:T(8,128)(2,1)S(1)}, u32[]{:S(2)}, u32[]{:S(2)}) %collective-permute-start.4) | collective-permute-done | bytes 69664 | tf_op jit(solution)/shard_map/ppermute | solution.py:139
  18.2 0.0 collective-permute-done.3.refs_4_
  18.2 0.3 %score.1 = (bf16[8,16,2176]{2,1,0:T(8,128)(2,1)S(1)}, f32[128,128]{1,0:T(8,128)S(1)}) custom-call(bf16[1,16,2176]{2,1,0:T(8,128)(2,1)S(1)} %bitcast.5, bf16[1,16,2176]{2,1,0:T(8,128)(2,1)S(1)} %collective-permute-done.refs_1_, bf16[1,16,2176]{2,1,0:T(8,128)(2,1)S(1)} %collective-permute-done.1.refs_2_, ...), custom_call_target="tpu_custom_call" | custom-call | tf_op jit(solution)/shard_map/score/pallas_call | solution.py:173
  18.5 0.0 copy-start
  18.6 0.1 collective-permute-start.6
  18.6 1.2 %collective-permute-done.6.other_ref = f32[128,128]{1,0:T(8,128)S(1)} collective-permute-done((f32[128,128]{1,0:T(8,128)S(1)}, f32[128,128]{1,0:T(8,128)S(1)}, u32[]{:S(2)}, u32[]{:S(2)}) %collective-permute-start.6) | collective-permute-done | bytes 65568 | tf_op jit(solution)/shard_map/ppermute | solution.py:184
  19.9 0.0 copy-done
  19.9 1.8 %finish.1 = (f32[8,2048]{1,0:T(8,128)}, f32[8,2048]{1,0:T(8,128)}, f32[8]{0:T(128)}) custom-call(s32[8]{0:T(128)S(1)} %copy-done, f32[128,128]{1,0:T(8,128)S(1)} %get-tuple-element.5.own_ref, f32[128,128]{1,0:T(8,128)S(1)} %collective-permute-done.6.other_ref, bf16[8,16,2176]{2,1,0:T(8,128)(2,1)S(1)} %get-tuple-element.6.all_ref), custom_call_target="tpu_custom_call" | custom-call | tf_op jit(solution)/shard_map/finish/pallas_call | solution.py:185
  (1 shorter events, 0.0 us)
Async XLA Ops:
  1.7 7.9 %collective-permute-start = (bf16[1,16,2176]{2,1,0:T(8,128)(2,1)S(1)}, bf16[1,16,2176]{2,1,0:T(8,128)(2,1)S(1)}, u32[]{:S(2)}, u32[]{:S(2)}) collective-permute-start(bf16[1,16,2176]{2,1,0:T(8,128)(2,1)S(1)} %bitcast.1), channel_id=1, source_target_pairs={{0,8},{1,9},{2,10},{3,11},{4,12},{5,13},{6,14},{7,15},{8,0},{9,1},... | collective-permute-start | bytes 208904 | tf_op jit(solution)/shard_map/ppermute | solution.py:139
  9.7 8.5 %collective-permute-start.3 = (bf16[2,16,2176]{2,1,0:T(8,128)(2,1)S(1)}, bf16[2,16,2176]{2,1,0:T(8,128)(2,1)S(1)}, u32[]{:S(2)}, u32[]{:S(2)}) collective-permute-start(bf16[2,16,2176]{2,1,0:T(8,128)(2,1)S(1)} %pad_maximum_fusion), channel_id=1, source_target_pairs={{0,6},{1,7},{2,4},{3,5},{4,2},{5,3},{6,0},{7,1},{8,14},{9,15},{10,... | collective-permute-start | bytes 417800 | tf_op jit(solution)/shard_map/ppermute | solution.py:139
  11.3 6.1 %collective-permute-start.2 = (bf16[1,16,2176]{2,1,0:T(8,128)(2,1)S(1)}, bf16[1,16,2176]{2,1,0:T(8,128)(2,1)S(1)}, u32[]{:S(2)}, u32[]{:S(2)}) collective-permute-start(bf16[1,16,2176]{2,1,0:T(8,128)(2,1)S(1)} %bitcast.3), channel_id=1, source_target_pairs={{0,2},{1,3},{2,0},{3,1},{4,6},{5,7},{6,4},{7,5},{8,10},{9,11},{10,... | collective-permute-start | bytes 208904 | tf_op jit(solution)/shard_map/ppermute | solution.py:139
  11.8 5.6 %collective-permute-start.1 = (bf16[1,16,2176]{2,1,0:T(8,128)(2,1)S(1)}, bf16[1,16,2176]{2,1,0:T(8,128)(2,1)S(1)}, u32[]{:S(2)}, u32[]{:S(2)}) collective-permute-start(bf16[1,16,2176]{2,1,0:T(8,128)(2,1)S(1)} %bitcast.4), channel_id=1, source_target_pairs={{0,4},{1,5},{2,6},{3,7},{4,0},{5,1},{6,2},{7,3},{8,12},{9,13},{10,... | collective-permute-start | bytes 208904 | tf_op jit(solution)/shard_map/ppermute | solution.py:139
  13.2 4.7 %collective-permute-start.5 = (bf16[1,16,2176]{2,1,0:T(8,128)(2,1)S(1)}, bf16[1,16,2176]{2,1,0:T(8,128)(2,1)S(1)}, u32[]{:S(2)}, u32[]{:S(2)}) collective-permute-start(bf16[1,16,2176]{2,1,0:T(8,128)(2,1)S(1)} %collective-permute-done.refs_1_), channel_id=1, source_target_pairs={{0,4},{1,5},{2,6},{3,7},{4,0},{5,1},{6,2},{7,3},{8,12},{9,13},{10,... | collective-permute-start | bytes 208904 | tf_op jit(solution)/shard_map/ppermute | solution.py:139
  13.8 4.3 %collective-permute-start.4 = (bf16[1,16,2176]{2,1,0:T(8,128)(2,1)S(1)}, bf16[1,16,2176]{2,1,0:T(8,128)(2,1)S(1)}, u32[]{:S(2)}, u32[]{:S(2)}) collective-permute-start(bf16[1,16,2176]{2,1,0:T(8,128)(2,1)S(1)} %collective-permute-done.refs_1_), channel_id=1, source_target_pairs={{0,2},{1,3},{2,0},{3,1},{4,6},{5,7},{6,4},{7,5},{8,10},{9,11},{10,... | collective-permute-start | bytes 208904 | tf_op jit(solution)/shard_map/ppermute | solution.py:139
  18.5 1.3 %copy-start = (s32[8]{0:T(128)S(1)}, s32[8]{0:T(128)}, u32[]{:S(2)}) copy-start(s32[8]{0:T(128)} %positive_ref.1) | copy-start | bytes 100
  18.6 1.3 %collective-permute-start.6 = (f32[128,128]{1,0:T(8,128)S(1)}, f32[128,128]{1,0:T(8,128)S(1)}, u32[]{:S(2)}, u32[]{:S(2)}) collective-permute-start(f32[128,128]{1,0:T(8,128)S(1)} %get-tuple-element.5.own_ref), channel_id=1, source_target_pairs={{0,1},{1,0},{2,3},{3,2},{4,5},{5,4},{6,7},{7,6},{8,9},{9,8},{10,11... | collective-permute-start | bytes 196616 | tf_op jit(solution)/shard_map/ppermute | solution.py:184

commit v3 on v2

--- a/solution.py
+++ b/solution.py
@@ -10,6 +10,7 @@
 
 sharpness_divisor = 0.05
 hardness_multiplier = 3.0
+scale = 1.0 / sharpness_divisor
 LANES = 128
 VMEM = pl.BlockSpec(memory_space=pltpu.VMEM)
 SMEM = pl.BlockSpec(memory_space=pltpu.SMEM)
@@ -28,7 +29,17 @@
 
 
 def pack_kernel(
-    positive_hbm, query_hbm, doc_hbm, hard_hbm, out_ref, positive_ref, query_ref, doc_ref, hard_ref, sems
+    positive_hbm,
+    query_hbm,
+    doc_hbm,
+    hard_hbm,
+    out_ref,
+    hit_ref,
+    positive_ref,
+    query_ref,
+    doc_ref,
+    hard_ref,
+    sems,
 ):
     copies = [
         pltpu.make_async_copy(source, target, sems.at[n])
@@ -48,6 +59,7 @@
     rows, width = query_ref.shape
     tail = out_ref.shape[1] - width
     hit = slot_matrix(positive_ref, rows)
+    hit_ref[...] = hit
     queries = jnp.dot(
         hit.astype(jnp.bfloat16),
         query_ref[...].astype(jnp.bfloat16),
@@ -69,65 +81,119 @@
 
 
 def score_kernel(masks, width, *refs):
-    *block_refs, all_ref, score_ref = refs
+    *block_refs, all_ref, score_ref, hold = refs
     me = lax.axis_index("row")
     side = lax.axis_index("col")
     for ref, (first, second) in zip(block_refs, masks):
         for n, (a, b) in enumerate(zip(first, second)):
             mask = a if a == b else jnp.where(side == 0, a, b)
-            value = ref[...] if len(ref.shape) == 2 else ref[n]
-            all_ref[lax.bitwise_xor(me, mask)] = value
+            all_ref[lax.bitwise_xor(me, mask)] = ref[n]
     blocks, height, depth = all_ref.shape
-    rows = all_ref[...].reshape(blocks * height, depth)[:, :width]
-    score_ref[...] = lax.dot_general(
-        rows, rows, (((1,), (1,)), ((), ())), preferred_element_type=jnp.float32
-    )
-
-
-def finish_kernel(
-    width, positive_ref, own_ref, other_ref, all_ref, request_ref, passage_ref, loss_ref, hold
-):
+    rows = height // 2
+    values = all_ref[...].reshape(blocks * height, depth)[:, :width]
+    product = lax.dot_general(
+        values, values, (((1,), (1,)), ((), ())), preferred_element_type=jnp.float32
+    ).reshape(blocks, height, blocks * height)
+    hold[...] = product
+    score_ref[: blocks * rows] = product[:, rows:].reshape(blocks * rows, blocks * height)
+    score_ref[blocks * rows :] = hold[me, :rows]
+
+
+def bias_kernel(width, hit_ref, all_ref, turned_ref, mine_ref, request_ref, passage_ref, hold):
     me = lax.axis_index("row")
     blocks, height, depth = all_ref.shape
     rows, total = height // 2, blocks * height
-    scores = (own_ref[...] + other_ref[...]) / sharpness_divisor
-    counts = all_ref[...].reshape(total, depth)[:, width:].astype(jnp.float32)
+    counts = all_ref[...].reshape(total, depth)[:, width : width + total].astype(jnp.float32)
     row = lax.broadcasted_iota(jnp.int32, (total, total), 0)
     lane = lax.broadcasted_iota(jnp.int32, (total, total), 1)
-    is_document = lax.rem(lane, height) >= rows
-    logits = jnp.where(
-        is_document & (row != lane), scores + jnp.log1p(hardness_multiplier * counts), -jnp.inf
-    ).reshape(blocks, 2, rows, total)
-    peak = jnp.max(jnp.max(logits, axis=1), axis=-1, keepdims=True)
-    mass = jnp.sum(jnp.sum(jnp.exp(logits - peak[:, None]), axis=1), axis=-1, keepdims=True)
-    lse = peak + jnp.log(mass)
-    weights = jnp.exp(logits - lse[:, None]).reshape(total, total)
-    hold[0] = weights.reshape(blocks, height, total)
-    hold[1] = weights.T.reshape(blocks, height, total)
-    hold[2] = logits.reshape(blocks, height, total)
-    hit = slot_matrix(positive_ref, rows)
-    back = hit.T.astype(jnp.bfloat16)
-    mine = hold[0, me].astype(jnp.bfloat16)
-    onto = hold[1, me].astype(jnp.bfloat16)
-    request_weights = jnp.dot(back, mine[:rows], preferred_element_type=jnp.float32).astype(jnp.bfloat16)
-    left = jnp.concatenate([request_weights, mine[rows:], onto], axis=0)
-    values = all_ref[...].reshape(total, depth)[:, :width]
-    product = jnp.dot(left, values, preferred_element_type=jnp.float32)
+    bias = jnp.where(
+        (lax.rem(lane, height) >= rows) & (row != lane),
+        jnp.log1p(hardness_multiplier * counts),
+        -jnp.inf,
+    )
+    hold[...] = bias.reshape(blocks, height, total)
+    mine_ref[...] = hold[me]
+    turned_ref[...] = bias.T.reshape(blocks, height, total)[:, rows:].reshape(blocks * rows, total)
     block = all_ref[me]
+    back = hit_ref[...].T.astype(jnp.bfloat16)
     anchors = jnp.dot(back, block[rows:, :width], preferred_element_type=jnp.float32)
-    request_ref[...] = (product[:rows] - anchors) / sharpness_divisor
-    passage_ref[...] = (
-        product[rows : 2 * rows] + product[3 * rows :] - block[:rows, :width].astype(jnp.float32)
-    ) / sharpness_divisor
-    own_logits = hold[2, me][:rows]
-    slot = lax.broadcasted_iota(jnp.int32, (rows, total), 0) + me * height + rows
+    request_ref[...] = anchors * -scale
+    passage_ref[...] = block[:rows, :width].astype(jnp.float32) * -scale
+
+
+def finish_kernel(
+    width,
+    pieces,
+    hit_ref,
+    own_ref,
+    other_ref,
+    turned_ref,
+    mine_ref,
+    request_base,
+    passage_base,
+    all_ref,
+    request_hbm,
+    passage_hbm,
+    loss_hbm,
+    request_ref,
+    passage_ref,
+    loss_ref,
+    sems,
+):
+    me = lax.axis_index("row")
+    blocks, height, _ = all_ref.shape
+    rows, total = height // 2, blocks * height
+    documents = blocks * rows
+    turned = (own_ref[:documents] + other_ref[:documents]) * scale + turned_ref[...]
+    is_document = lax.rem(lax.broadcasted_iota(jnp.int32, (1, total), 1), height) >= rows
+
+    def partner(value):
+        return jnp.where(
+            is_document, jnp.roll(value, rows, axis=1), jnp.roll(value, -rows, axis=1)
+        )
+
+    top = jnp.max(turned, axis=0, keepdims=True)
+    top = jnp.maximum(top, partner(top))
+    mass = jnp.sum(jnp.exp(turned - top), axis=0, keepdims=True)
+    lse = top + jnp.log(mass + partner(mass))
     at = lax.broadcasted_iota(jnp.int32, (rows, total), 1)
-    picked = jnp.sum(jnp.where(slot == at, own_logits, 0.0), axis=1, keepdims=True)
-    again = jnp.max(hold[2, me].reshape(2, rows, total), axis=0)
-    top = jnp.max(again, axis=1, keepdims=True)
-    spread = jnp.exp(hold[2, me].reshape(2, rows, total) - top[None])
-    own_lse = top + jnp.log(jnp.sum(jnp.sum(spread, axis=0), axis=1, keepdims=True))
-    loss_ref[...] = jnp.sum(hit * (own_lse - picked), axis=0)
+    slot = lax.broadcasted_iota(jnp.int32, (rows, total), 0) + me * height
+    own_lse = jnp.sum(jnp.where(at == slot, lse, 0.0), axis=1, keepdims=True)
+    ours = pl.ds(pl.multiple_of(me * rows, rows), rows)
+    query_logits = (own_ref[documents:] + other_ref[documents:]) * scale + mine_ref[:rows]
+    document_scores = (own_ref[ours] + other_ref[ours]) * scale
+    query_weights = jnp.exp(query_logits - own_lse)
+    document_weights = jnp.exp(document_scores + mine_ref[rows:] - own_lse)
+    onto = jnp.exp(document_scores + turned_ref[ours] - lse)
+    back = hit_ref[...].T.astype(jnp.bfloat16)
+    request_weights = jnp.dot(
+        back, query_weights.astype(jnp.bfloat16), preferred_element_type=jnp.float32
+    )
+    left = jnp.concatenate(
+        [request_weights, document_weights, onto, jnp.zeros_like(onto)], axis=0
+    ).astype(jnp.bfloat16)
+    picked = jnp.sum(jnp.where(at == slot + rows, query_logits, 0.0), axis=1, keepdims=True)
+    loss_ref[...] = jnp.sum(hit_ref[...] * (own_lse - picked), axis=0)
+    copies = [pltpu.make_async_copy(loss_ref, loss_hbm, sems.at[2 * pieces])]
+    copies[0].start()
+    step = width // pieces
+    for n in range(pieces):
+        span = pl.ds(n * step, step)
+        values = all_ref[:, :, span].reshape(total, step)
+        product = jnp.dot(left, values, preferred_element_type=jnp.float32)
+        request_ref[:, span] = product[:rows] * scale + request_base[:, span]
+        passage_ref[:, span] = (
+            product[rows : 2 * rows] + product[2 * rows : 3 * rows]
+        ) * scale + passage_base[:, span]
+        for k, (source, target) in enumerate(
+            ((request_ref, request_hbm), (passage_ref, passage_hbm))
+        ):
+            copies.append(
+                pltpu.make_async_copy(source.at[:, span], target.at[:, span], sems.at[2 * n + k])
+            )
+            copies[-1].start()
+    for copy in copies:
+        copy.wait()
 
 
 def exchange(value, masks):
@@ -139,6 +205,7 @@
     return lax.ppermute(value, ("row", "col"), pairs)
 
 
+PIECES = 4
 PLAN = [((0,), (4, 4)), ((0,), (2, 2)), ((0,), (1, 1)), ((0, 1), (3, 3)), ((1,), (1, 1)), ((1,), (2, 2))]
 
 
@@ -147,11 +214,14 @@
     count = lax.axis_size("row")
     height, total = 2 * rows, 2 * rows * count
     tail = -(-total // LANES) * LANES
-    block = pl.pallas_call(
+    block, hit = pl.pallas_call(
         pack_kernel,
-        out_shape=jax.ShapeDtypeStruct((height, width + tail), jnp.bfloat16),
+        out_shape=(
+            jax.ShapeDtypeStruct((height, width + tail), jnp.bfloat16),
+            jax.ShapeDtypeStruct((rows, rows), jnp.float32),
+        ),
         in_specs=[HBM, HBM, HBM, HBM],
-        out_specs=VMEM,
+        out_specs=(VMEM, VMEM),
         scratch_shapes=[
             pltpu.SMEM(positive.shape, positive.dtype),
             pltpu.VMEM(queries.shape, queries.dtype),
@@ -174,27 +244,47 @@
         functools.partial(score_kernel, masks, width),
         out_shape=(
             jax.ShapeDtypeStruct((count, height, width + tail), jnp.bfloat16),
-            jax.ShapeDtypeStruct((total, total), jnp.float32),
+            jax.ShapeDtypeStruct((total // 2 + rows, total), jnp.float32),
         ),
         in_specs=[VMEM] * len(pieces),
         out_specs=(VMEM, VMEM),
+        scratch_shapes=[pltpu.VMEM((count, height, total), jnp.float32)],
         compiler_params=PARAMS,
         name="score",
     )(*pieces)
     other = lax.ppermute(own, "col", [(0, 1), (1, 0)])
+    turned, mine, request_base, passage_base = pl.pallas_call(
+        functools.partial(bias_kernel, width),
+        out_shape=(
+            jax.ShapeDtypeStruct((total // 2, total), jnp.float32),
+            jax.ShapeDtypeStruct((height, total), jnp.float32),
+            jax.ShapeDtypeStruct((rows, width), jnp.float32),
+            jax.ShapeDtypeStruct((rows, width), jnp.float32),
+        ),
+        in_specs=[VMEM, VMEM],
+        out_specs=(VMEM, VMEM, VMEM, VMEM),
+        scratch_shapes=[pltpu.VMEM((count, height, total), jnp.float32)],
+        compiler_params=PARAMS,
+        name="bias",
+    )(hit, everything)
     return pl.pallas_call(
-        functools.partial(finish_kernel, width),
+        functools.partial(finish_kernel, width, PIECES),
         out_shape=(
             jax.ShapeDtypeStruct((rows, width), jnp.float32),
             jax.ShapeDtypeStruct((rows, width), jnp.float32),
             jax.ShapeDtypeStruct((rows,), jnp.float32),
         ),
-        in_specs=[SMEM, VMEM, VMEM, VMEM],
-        out_specs=(VMEM, VMEM, VMEM),
-        scratch_shapes=[pltpu.VMEM((3, count, height, total), jnp.float32)],
+        in_specs=[VMEM] * 8,
+        out_specs=(HBM, HBM, HBM),
+        scratch_shapes=[
+            pltpu.VMEM((rows, width), jnp.float32),
+            pltpu.VMEM((rows, width), jnp.float32),
+            pltpu.VMEM((rows,), jnp.float32),
+            pltpu.SemaphoreType.DMA((2 * PIECES + 1,)),
+        ],
         compiler_params=PARAMS,
         name="finish",
-    )(positive, own, other, everything)
+    )(hit, own, other, turned, mine, request_base, passage_base, everything)
 
 
 def weigh(request_similarity, passage_similarity, positive, hard_ids, batch_size):

time: 21.8 us -> 21.2 us (0.972)
  Pallas kernels: 3.25 us -> 2.91 us
  waiting for transfers between devices: 7.86 us -> 7.63 us
    pallas_call x2 -> x3, Pallas kernels: 2.91 us -> 2.56 us  [the longest x1 1.27 us: on_device_fast(): pl.pallas_call(functools.partial(finish_kernel, width, PIECES), out_shape...]
    ppermute x1, waiting for transfers between devices: 1.24 us -> 1 us  [on_device_fast(): other = lax.ppermute(own, 'col', [(0, 1), (1, 0)])]
  transfers between devices with their start and end apart: 7 -> 7, of which waited for: 5 -> 5; matrix products, arithmetic and copies ran while one was open for 0% -> 0% of each run, Pallas kernels for 0% -> 1%
where the time goes in v3:
time: 21.2 us; the launch traced here: 21.1 us
  starting transfers between devices  9.86 us (47%)
  waiting for transfers between devices  7.63 us (36%)
  Pallas kernels  2.91 us (14%)
  between operations  0.67 us (3%)
    ppermute x6, starting transfers between devices, exchange(): return lax.ppermute(value, ('row', 'col'), pairs)  9.79 us
    ppermute x6, waiting for transfers between devices, exchange(): return lax.ppermute(value, ('row', 'col'), pairs)  6.62 us
    pallas_call x1, Pallas kernels, on_device_fast(): pl.pallas_call(functools.partial(finish_kernel, width, PIECES), out_shape...  1.27 us
    pallas_call x1, Pallas kernels, on_device_fast(): pl.pallas_call(pack_kernel, out_shape=(jax.ShapeDtypeStruct((height, widt...  1.11 us
    ppermute x1, waiting for transfers between devices, on_device_fast(): other = lax.ppermute(own, 'col', [(0, 1), (1, 0)])  1 us
  transfers between devices with their start and end apart: 7, of which 5 were waited for; matrix products, arithmetic and copies ran while one was open for 0% of the time, Pallas kernels for 1%

profile of v3, /device:TPU:0, one launch (start us, length us, event | category | flops | bytes accessed | tf_op | source)
XLA Modules:
  0.0 21.1 jit_solution(12856310997419081129)
XLA Ops:
  0.6 1.1 %pack.1 = (bf16[16,2176]{1,0:T(8,128)(2,1)S(1)}, f32[8,8]{1,0:T(8,128)S(1)}) custom-call(s32[8]{0:T(128)} %positive_hbm.1, f32[8,2048]{1,0:T(8,128)} %query_hbm.1, f32[8,2048]{1,0:T(8,128)} %doc_hbm.1, s32[8,7]{1,0:T(8,128)} %hard_hbm.1), custom_call_target="tpu_custom_call" | custom-call | tf_op jit(solution)/shard_map/pack/pallas_call | solution.py:217
  1.7 4.1 %collective-permute-start = (bf16[1,16,2176]{2,1,0:T(8,128)(2,1)S(1)}, bf16[1,16,2176]{2,1,0:T(8,128)(2,1)S(1)}, u32[]{:S(2)}, u32[]{:S(2)}) collective-permute-start(bf16[1,16,2176]{2,1,0:T(8,128)(2,1)S(1)} %bitcast.1), channel_id=1, source_target_pairs={{0,8},{1,9},{2,10},{3,11},{4,12},{5,13},{6,14},{7,15},{8,0},{9,1},... | collective-permute-start | bytes 208904 | tf_op jit(solution)/shard_map/ppermute | solution.py:205
  5.9 3.8 %collective-permute-done.refs_1_ = bf16[1,16,2176]{2,1,0:T(8,128)(2,1)S(1)} collective-permute-done((bf16[1,16,2176]{2,1,0:T(8,128)(2,1)S(1)}, bf16[1,16,2176]{2,1,0:T(8,128)(2,1)S(1)}, u32[]{:S(2)}, u32[]{:S(2)}) %collective-permute-start) | collective-permute-done | bytes 69664 | tf_op jit(solution)/shard_map/ppermute | solution.py:205
  9.7 1.6 %collective-permute-start.3 = (bf16[2,16,2176]{2,1,0:T(8,128)(2,1)S(1)}, bf16[2,16,2176]{2,1,0:T(8,128)(2,1)S(1)}, u32[]{:S(2)}, u32[]{:S(2)}) collective-permute-start(bf16[2,16,2176]{2,1,0:T(8,128)(2,1)S(1)} %pad_maximum_fusion), channel_id=1, source_target_pairs={{0,6},{1,7},{2,4},{3,5},{4,2},{5,3},{6,0},{7,1},{8,14},{9,15},{10,... | collective-permute-start | bytes 417800 | tf_op jit(solution)/shard_map/ppermute | solution.py:205
  11.3 0.5 %collective-permute-start.2 = (bf16[1,16,2176]{2,1,0:T(8,128)(2,1)S(1)}, bf16[1,16,2176]{2,1,0:T(8,128)(2,1)S(1)}, u32[]{:S(2)}, u32[]{:S(2)}) collective-permute-start(bf16[1,16,2176]{2,1,0:T(8,128)(2,1)S(1)} %bitcast.3), channel_id=1, source_target_pairs={{0,2},{1,3},{2,0},{3,1},{4,6},{5,7},{6,4},{7,5},{8,10},{9,11},{10,... | collective-permute-start | bytes 208904 | tf_op jit(solution)/shard_map/ppermute | solution.py:205
  11.8 1.4 %collective-permute-start.1 = (bf16[1,16,2176]{2,1,0:T(8,128)(2,1)S(1)}, bf16[1,16,2176]{2,1,0:T(8,128)(2,1)S(1)}, u32[]{:S(2)}, u32[]{:S(2)}) collective-permute-start(bf16[1,16,2176]{2,1,0:T(8,128)(2,1)S(1)} %bitcast.4), channel_id=1, source_target_pairs={{0,4},{1,5},{2,6},{3,7},{4,0},{5,1},{6,2},{7,3},{8,12},{9,13},{10,... | collective-permute-start | bytes 208904 | tf_op jit(solution)/shard_map/ppermute | solution.py:205
  13.2 0.6 %collective-permute-start.5 = (bf16[1,16,2176]{2,1,0:T(8,128)(2,1)S(1)}, bf16[1,16,2176]{2,1,0:T(8,128)(2,1)S(1)}, u32[]{:S(2)}, u32[]{:S(2)}) collective-permute-start(bf16[1,16,2176]{2,1,0:T(8,128)(2,1)S(1)} %collective-permute-done.refs_1_), channel_id=1, source_target_pairs={{0,4},{1,5},{2,6},{3,7},{4,0},{5,1},{6,2},{7,3},{8,12},{9,13},{10,... | collective-permute-start | bytes 208904 | tf_op jit(solution)/shard_map/ppermute | solution.py:205
  13.8 1.5 %collective-permute-start.4 = (bf16[1,16,2176]{2,1,0:T(8,128)(2,1)S(1)}, bf16[1,16,2176]{2,1,0:T(8,128)(2,1)S(1)}, u32[]{:S(2)}, u32[]{:S(2)}) collective-permute-start(bf16[1,16,2176]{2,1,0:T(8,128)(2,1)S(1)} %collective-permute-done.refs_1_), channel_id=1, source_target_pairs={{0,2},{1,3},{2,0},{3,1},{4,6},{5,7},{6,4},{7,5},{8,10},{9,11},{10,... | collective-permute-start | bytes 208904 | tf_op jit(solution)/shard_map/ppermute | solution.py:205
  15.3 2.1 %collective-permute-done.2.refs_3_ = bf16[1,16,2176]{2,1,0:T(8,128)(2,1)S(1)} collective-permute-done((bf16[1,16,2176]{2,1,0:T(8,128)(2,1)S(1)}, bf16[1,16,2176]{2,1,0:T(8,128)(2,1)S(1)}, u32[]{:S(2)}, u32[]{:S(2)}) %collective-permute-start.2) | collective-permute-done | bytes 69664 | tf_op jit(solution)/shard_map/ppermute | solution.py:205
  17.4 0.0 collective-permute-done.1.refs_2_
  17.4 0.6 %collective-permute-done.5.refs_6_ = bf16[1,16,2176]{2,1,0:T(8,128)(2,1)S(1)} collective-permute-done((bf16[1,16,2176]{2,1,0:T(8,128)(2,1)S(1)}, bf16[1,16,2176]{2,1,0:T(8,128)(2,1)S(1)}, u32[]{:S(2)}, u32[]{:S(2)}) %collective-permute-start.5) | collective-permute-done | bytes 69664 | tf_op jit(solution)/shard_map/ppermute | solution.py:205
  18.0 0.2 %collective-permute-done.4.refs_5_ = bf16[1,16,2176]{2,1,0:T(8,128)(2,1)S(1)} collective-permute-done((bf16[1,16,2176]{2,1,0:T(8,128)(2,1)S(1)}, bf16[1,16,2176]{2,1,0:T(8,128)(2,1)S(1)}, u32[]{:S(2)}, u32[]{:S(2)}) %collective-permute-start.4) | collective-permute-done | bytes 69664 | tf_op jit(solution)/shard_map/ppermute | solution.py:205
  18.2 0.0 collective-permute-done.3.refs_4_
  18.2 0.3 %score.1 = (bf16[8,16,2176]{2,1,0:T(8,128)(2,1)S(1)}, f32[72,128]{1,0:T(8,128)S(1)}) custom-call(bf16[1,16,2176]{2,1,0:T(8,128)(2,1)S(1)} %bitcast.5, bf16[1,16,2176]{2,1,0:T(8,128)(2,1)S(1)} %collective-permute-done.refs_1_, bf16[1,16,2176]{2,1,0:T(8,128)(2,1)S(1)} %collective-permute-done.1.refs_2_, ...), custom_call_target="tpu_custom_call" | custom-call | tf_op jit(solution)/shard_map/score/pallas_call | solution.py:243
  18.5 0.1 collective-permute-start.6
  18.6 0.2 bias.1
  18.8 1.0 %collective-permute-done.6.other_ref = f32[72,128]{1,0:T(8,128)S(1)} collective-permute-done((f32[72,128]{1,0:T(8,128)S(1)}, f32[72,128]{1,0:T(8,128)S(1)}, u32[]{:S(2)}, u32[]{:S(2)}) %collective-permute-start.6) | collective-permute-done | bytes 36896 | tf_op jit(solution)/shard_map/ppermute | solution.py:255
  19.8 1.3 %finish.1 = (f32[8,2048]{1,0:T(8,128)}, f32[8,2048]{1,0:T(8,128)}, f32[8]{0:T(128)}) custom-call(f32[8,8]{1,0:T(8,128)S(1)} %get-tuple-element.11.hit_ref, f32[72,128]{1,0:T(8,128)S(1)} %get-tuple-element.13.own_ref, f32[72,128]{1,0:T(8,128)S(1)} %collective-permute-done.6.other_ref, f32[64,128]{1,0:T(8,128)S(1)} %get-tuple-element.15.turned_ref, ...), custom_call_target="tpu_custom_call" | custom-call | tf_op jit(solution)/shard_map/finish/pallas_call | solution.py:270
  (1 shorter events, 0.0 us)
Async XLA Ops:
  1.7 7.9 %collective-permute-start = (bf16[1,16,2176]{2,1,0:T(8,128)(2,1)S(1)}, bf16[1,16,2176]{2,1,0:T(8,128)(2,1)S(1)}, u32[]{:S(2)}, u32[]{:S(2)}) collective-permute-start(bf16[1,16,2176]{2,1,0:T(8,128)(2,1)S(1)} %bitcast.1), channel_id=1, source_target_pairs={{0,8},{1,9},{2,10},{3,11},{4,12},{5,13},{6,14},{7,15},{8,0},{9,1},... | collective-permute-start | bytes 208904 | tf_op jit(solution)/shard_map/ppermute | solution.py:205
  9.7 8.5 %collective-permute-start.3 = (bf16[2,16,2176]{2,1,0:T(8,128)(2,1)S(1)}, bf16[2,16,2176]{2,1,0:T(8,128)(2,1)S(1)}, u32[]{:S(2)}, u32[]{:S(2)}) collective-permute-start(bf16[2,16,2176]{2,1,0:T(8,128)(2,1)S(1)} %pad_maximum_fusion), channel_id=1, source_target_pairs={{0,6},{1,7},{2,4},{3,5},{4,2},{5,3},{6,0},{7,1},{8,14},{9,15},{10,... | collective-permute-start | bytes 417800 | tf_op jit(solution)/shard_map/ppermute | solution.py:205
  11.3 6.1 %collective-permute-start.2 = (bf16[1,16,2176]{2,1,0:T(8,128)(2,1)S(1)}, bf16[1,16,2176]{2,1,0:T(8,128)(2,1)S(1)}, u32[]{:S(2)}, u32[]{:S(2)}) collective-permute-start(bf16[1,16,2176]{2,1,0:T(8,128)(2,1)S(1)} %bitcast.3), channel_id=1, source_target_pairs={{0,2},{1,3},{2,0},{3,1},{4,6},{5,7},{6,4},{7,5},{8,10},{9,11},{10,... | collective-permute-start | bytes 208904 | tf_op jit(solution)/shard_map/ppermute | solution.py:205
  11.8 5.6 %collective-permute-start.1 = (bf16[1,16,2176]{2,1,0:T(8,128)(2,1)S(1)}, bf16[1,16,2176]{2,1,0:T(8,128)(2,1)S(1)}, u32[]{:S(2)}, u32[]{:S(2)}) collective-permute-start(bf16[1,16,2176]{2,1,0:T(8,128)(2,1)S(1)} %bitcast.4), channel_id=1, source_target_pairs={{0,4},{1,5},{2,6},{3,7},{4,0},{5,1},{6,2},{7,3},{8,12},{9,13},{10,... | collective-permute-start | bytes 208904 | tf_op jit(solution)/shard_map/ppermute | solution.py:205
  13.2 4.7 %collective-permute-start.5 = (bf16[1,16,2176]{2,1,0:T(8,128)(2,1)S(1)}, bf16[1,16,2176]{2,1,0:T(8,128)(2,1)S(1)}, u32[]{:S(2)}, u32[]{:S(2)}) collective-permute-start(bf16[1,16,2176]{2,1,0:T(8,128)(2,1)S(1)} %collective-permute-done.refs_1_), channel_id=1, source_target_pairs={{0,4},{1,5},{2,6},{3,7},{4,0},{5,1},{6,2},{7,3},{8,12},{9,13},{10,... | collective-permute-start | bytes 208904 | tf_op jit(solution)/shard_map/ppermute | solution.py:205
  13.8 4.3 %collective-permute-start.4 = (bf16[1,16,2176]{2,1,0:T(8,128)(2,1)S(1)}, bf16[1,16,2176]{2,1,0:T(8,128)(2,1)S(1)}, u32[]{:S(2)}, u32[]{:S(2)}) collective-permute-start(bf16[1,16,2176]{2,1,0:T(8,128)(2,1)S(1)} %collective-permute-done.refs_1_), channel_id=1, source_target_pairs={{0,2},{1,3},{2,0},{3,1},{4,6},{5,7},{6,4},{7,5},{8,10},{9,11},{10,... | collective-permute-start | bytes 208904 | tf_op jit(solution)/shard_map/ppermute | solution.py:205
  18.5 1.3 %collective-permute-start.6 = (f32[72,128]{1,0:T(8,128)S(1)}, f32[72,128]{1,0:T(8,128)S(1)}, u32[]{:S(2)}, u32[]{:S(2)}) collective-permute-start(f32[72,128]{1,0:T(8,128)S(1)} %get-tuple-element.13.own_ref), channel_id=1, source_target_pairs={{0,1},{1,0},{2,3},{3,2},{4,5},{5,4},{6,7},{7,6},{8,9},{9,8},{10,11... | collective-permute-start | bytes 110600 | tf_op jit(solution)/shard_map/ppermute | solution.py:255

commit v4 on v3

--- a/solution.py
+++ b/solution.py
@@ -60,11 +60,6 @@
     tail = out_ref.shape[1] - width
     hit = slot_matrix(positive_ref, rows)
     hit_ref[...] = hit
-    queries = jnp.dot(
-        hit.astype(jnp.bfloat16),
-        query_ref[...].astype(jnp.bfloat16),
-        preferred_element_type=jnp.float32,
-    )
     lane = lax.broadcasted_iota(jnp.int32, (rows, tail), 1)
     block, place = lane // (2 * rows), lax.rem(lane, 2 * rows)
     column = jnp.where(place >= rows, block * rows + place - rows, -1)
@@ -72,79 +67,72 @@
     counts = jnp.zeros((rows, tail), jnp.float32)
     for k in range(hard.shape[1]):
         counts = counts + jnp.where(hard[:, k][:, None] == column, 1.0, 0.0)
-    counts = jnp.dot(
-        hit.astype(jnp.bfloat16), counts.astype(jnp.bfloat16), preferred_element_type=jnp.float32
-    )
-    upper = jnp.concatenate([queries, counts], axis=1)
+    raw = jnp.concatenate([query_ref[...], counts], axis=1)
+    upper = jnp.zeros_like(raw)
+    for i in range(rows):
+        upper = jnp.where(hit[:, i][:, None] > 0.0, raw[i][None, :], upper)
     lower = jnp.concatenate([doc_ref[...], jnp.zeros((rows, tail), jnp.float32)], axis=1)
     out_ref[...] = jnp.concatenate([upper, lower], axis=0).astype(jnp.bfloat16)
 
 
-def score_kernel(masks, width, *refs):
-    *block_refs, all_ref, score_ref, hold = refs
-    me = lax.axis_index("row")
-    side = lax.axis_index("col")
-    for ref, (first, second) in zip(block_refs, masks):
-        for n, (a, b) in enumerate(zip(first, second)):
-            mask = a if a == b else jnp.where(side == 0, a, b)
-            all_ref[lax.bitwise_xor(me, mask)] = ref[n]
-    blocks, height, depth = all_ref.shape
-    rows = height // 2
-    values = all_ref[...].reshape(blocks * height, depth)[:, :width]
+def stack(refs, places, start, stop):
+    return jnp.concatenate([refs[p][n, :, start:stop] for p, n in places], axis=0)
+
+
+def score_kernel(places, width, *refs):
+    *block_refs, score_ref = refs
+    values = stack(block_refs, places, 0, width)
     product = lax.dot_general(
         values, values, (((1,), (1,)), ((), ())), preferred_element_type=jnp.float32
-    ).reshape(blocks, height, blocks * height)
-    hold[...] = product
-    score_ref[: blocks * rows] = product[:, rows:].reshape(blocks * rows, blocks * height)
-    score_ref[blocks * rows :] = hold[me, :rows]
-
-
-def bias_kernel(width, hit_ref, all_ref, turned_ref, mine_ref, request_ref, passage_ref, hold):
+    )
+    height, blocks = block_refs[0].shape[1], len(places)
+    rows = height // 2
+    by_block = product.reshape(blocks, height, blocks * height)
+    score_ref[: blocks * rows] = by_block[:, rows:].reshape(blocks * rows, blocks * height)
+    score_ref[blocks * rows :] = product[:rows]
+
+
+def bias_kernel(places, width, hit_ref, *refs):
+    *block_refs, turned_ref, mine_ref, request_ref, passage_ref = refs
     me = lax.axis_index("row")
-    blocks, height, depth = all_ref.shape
+    height, blocks = block_refs[0].shape[1], len(places)
     rows, total = height // 2, blocks * height
-    counts = all_ref[...].reshape(total, depth)[:, width : width + total].astype(jnp.float32)
+    counts = stack(block_refs, places, width, width + total).astype(jnp.float32)
     row = lax.broadcasted_iota(jnp.int32, (total, total), 0)
     lane = lax.broadcasted_iota(jnp.int32, (total, total), 1)
+    bit = 1
+    while bit < blocks:
+        shift = bit * height
+        other = jnp.where(
+            (lane // shift) % 2 == 0,
+            jnp.roll(counts, -shift, axis=1),
+            jnp.roll(counts, shift, axis=1),
+        )
+        counts = jnp.where((me // bit) % 2 == 1, other, counts)
+        bit *= 2
     bias = jnp.where(
         (lax.rem(lane, height) >= rows) & (row != lane),
         jnp.log1p(hardness_multiplier * counts),
         -jnp.inf,
     )
-    hold[...] = bias.reshape(blocks, height, total)
-    mine_ref[...] = hold[me]
+    mine_ref[...] = bias[:height]
     turned_ref[...] = bias.T.reshape(blocks, height, total)[:, rows:].reshape(blocks * rows, total)
-    block = all_ref[me]
+    block = block_refs[0]
     back = hit_ref[...].T.astype(jnp.bfloat16)
-    anchors = jnp.dot(back, block[rows:, :width], preferred_element_type=jnp.float32)
+    anchors = jnp.dot(back, block[0, rows:, :width], preferred_element_type=jnp.float32)
     request_ref[...] = anchors * -scale
-    passage_ref[...] = block[:rows, :width].astype(jnp.float32) * -scale
-
-
-def finish_kernel(
-    width,
-    pieces,
-    hit_ref,
-    own_ref,
-    other_ref,
-    turned_ref,
-    mine_ref,
-    request_base,
-    passage_base,
-    all_ref,
-    request_hbm,
-    passage_hbm,
-    loss_hbm,
-    request_ref,
-    passage_ref,
-    loss_ref,
-    sems,
-):
-    me = lax.axis_index("row")
-    blocks, height, _ = all_ref.shape
+    passage_ref[...] = block[0, :rows, :width].astype(jnp.float32) * -scale
+
+
+def finish_kernel(places, width, pieces, *refs):
+    hit_ref, own_ref, other_ref, turned_ref, mine_ref, request_base, passage_base = refs[:7]
+    block_refs = refs[7:-7]
+    request_hbm, passage_hbm, loss_hbm, request_ref, passage_ref, loss_ref, sems = refs[-7:]
+    height, blocks = block_refs[0].shape[1], len(places)
     rows, total = height // 2, blocks * height
     documents = blocks * rows
-    turned = (own_ref[:documents] + other_ref[:documents]) * scale + turned_ref[...]
+    scores = (own_ref[...] + other_ref[...]) * scale
+    turned = scores[:documents] + turned_ref[...]
     is_document = lax.rem(lax.broadcasted_iota(jnp.int32, (1, total), 1), height) >= rows
 
     def partner(value):
@@ -157,14 +145,12 @@
     mass = jnp.sum(jnp.exp(turned - top), axis=0, keepdims=True)
     lse = top + jnp.log(mass + partner(mass))
     at = lax.broadcasted_iota(jnp.int32, (rows, total), 1)
-    slot = lax.broadcasted_iota(jnp.int32, (rows, total), 0) + me * height
+    slot = lax.broadcasted_iota(jnp.int32, (rows, total), 0)
     own_lse = jnp.sum(jnp.where(at == slot, lse, 0.0), axis=1, keepdims=True)
-    ours = pl.ds(pl.multiple_of(me * rows, rows), rows)
-    query_logits = (own_ref[documents:] + other_ref[documents:]) * scale + mine_ref[:rows]
-    document_scores = (own_ref[ours] + other_ref[ours]) * scale
+    query_logits = scores[documents:] + mine_ref[:rows]
     query_weights = jnp.exp(query_logits - own_lse)
-    document_weights = jnp.exp(document_scores + mine_ref[rows:] - own_lse)
-    onto = jnp.exp(document_scores + turned_ref[ours] - lse)
+    document_weights = jnp.exp(scores[:rows] + mine_ref[rows:] - own_lse)
+    onto = jnp.exp(turned[:rows] - lse)
     back = hit_ref[...].T.astype(jnp.bfloat16)
     request_weights = jnp.dot(
         back, query_weights.astype(jnp.bfloat16), preferred_element_type=jnp.float32
@@ -172,14 +158,11 @@
     left = jnp.concatenate(
         [request_weights, document_weights, onto, jnp.zeros_like(onto)], axis=0
     ).astype(jnp.bfloat16)
-    picked = jnp.sum(jnp.where(at == slot + rows, query_logits, 0.0), axis=1, keepdims=True)
-    loss_ref[...] = jnp.sum(hit_ref[...] * (own_lse - picked), axis=0)
-    copies = [pltpu.make_async_copy(loss_ref, loss_hbm, sems.at[2 * pieces])]
-    copies[0].start()
+    copies = []
     step = width // pieces
     for n in range(pieces):
         span = pl.ds(n * step, step)
-        values = all_ref[:, :, span].reshape(total, step)
+        values = stack(block_refs, places, n * step, (n + 1) * step)
         product = jnp.dot(left, values, preferred_element_type=jnp.float32)
         request_ref[:, span] = product[:rows] * scale + request_base[:, span]
         passage_ref[:, span] = (
@@ -192,21 +175,20 @@
                 pltpu.make_async_copy(source.at[:, span], target.at[:, span], sems.at[2 * n + k])
             )
             copies[-1].start()
+    picked = jnp.sum(jnp.where(at == slot + rows, query_logits, 0.0), axis=1, keepdims=True)
+    loss_ref[...] = jnp.sum(hit_ref[...] * (own_lse - picked), axis=0)
+    copies.append(pltpu.make_async_copy(loss_ref, loss_hbm, sems.at[2 * pieces]))
+    copies[-1].start()
     for copy in copies:
         copy.wait()
 
 
-def exchange(value, masks):
-    count = lax.axis_size("row")
-    sides = lax.axis_size("col")
-    pairs = [
-        (sides * i + c, sides * (i ^ masks[c]) + c) for i in range(count) for c in range(sides)
-    ]
-    return lax.ppermute(value, ("row", "col"), pairs)
+def exchange(value, mask):
+    return lax.ppermute(value, "row", [(i, i ^ mask) for i in range(lax.axis_size("row"))])
 
 
 PIECES = 4
-PLAN = [((0,), (4, 4)), ((0,), (2, 2)), ((0,), (1, 1)), ((0, 1), (3, 3)), ((1,), (1, 1)), ((1,), (2, 2))]
+PLAN = (((0,), 4), ((0,), 2), ((0,), 1), ((0, 1), 3), ((1,), 1), ((1,), 2))
 
 
 def on_device_fast(queries, documents, positive, hard_ids):
@@ -232,49 +214,44 @@
         compiler_params=PARAMS,
         name="pack",
     )(*(pltpu.with_memory_space_constraint(v, pltpu.HBM) for v in (positive, queries, documents, hard_ids)))
-    pieces, masks = [block[None]], [([0], [0])]
-    for sources, hops in PLAN:
+    pieces, distances = [block[None]], [[0]]
+    for sources, mask in PLAN:
         held = [pieces[n] for n in sources]
         held = held[0] if len(held) == 1 else jnp.concatenate(held, axis=0)
-        pieces.append(exchange(held, hops))
-        masks.append(
-            tuple([m ^ hops[c] for n in sources for m in masks[n][c]] for c in range(len(hops)))
-        )
-    everything, own = pl.pallas_call(
-        functools.partial(score_kernel, masks, width),
-        out_shape=(
-            jax.ShapeDtypeStruct((count, height, width + tail), jnp.bfloat16),
-            jax.ShapeDtypeStruct((total // 2 + rows, total), jnp.float32),
-        ),
+        pieces.append(exchange(held, mask))
+        distances.append([m ^ mask for n in sources for m in distances[n]])
+    where = {m: (p, n) for p, found in enumerate(distances) for n, m in enumerate(found)}
+    places = [where[m] for m in range(count)]
+    own = pl.pallas_call(
+        functools.partial(score_kernel, places, width),
+        out_shape=jax.ShapeDtypeStruct((total // 2 + rows, total), jnp.float32),
         in_specs=[VMEM] * len(pieces),
-        out_specs=(VMEM, VMEM),
-        scratch_shapes=[pltpu.VMEM((count, height, total), jnp.float32)],
+        out_specs=VMEM,
         compiler_params=PARAMS,
         name="score",
     )(*pieces)
     other = lax.ppermute(own, "col", [(0, 1), (1, 0)])
-    turned, mine, request_base, passage_base = pl.pallas_call(
-        functools.partial(bias_kernel, width),
+    prepared = pl.pallas_call(
+        functools.partial(bias_kernel, places, width),
         out_shape=(
             jax.ShapeDtypeStruct((total // 2, total), jnp.float32),
             jax.ShapeDtypeStruct((height, total), jnp.float32),
             jax.ShapeDtypeStruct((rows, width), jnp.float32),
             jax.ShapeDtypeStruct((rows, width), jnp.float32),
         ),
-        in_specs=[VMEM, VMEM],
+        in_specs=[VMEM] * (1 + len(pieces)),
         out_specs=(VMEM, VMEM, VMEM, VMEM),
-        scratch_shapes=[pltpu.VMEM((count, height, total), jnp.float32)],
         compiler_params=PARAMS,
         name="bias",
-    )(hit, everything)
+    )(hit, *pieces)
     return pl.pallas_call(
-        functools.partial(finish_kernel, width, PIECES),
+        functools.partial(finish_kernel, places, width, PIECES),
         out_shape=(
             jax.ShapeDtypeStruct((rows, width), jnp.float32),
             jax.ShapeDtypeStruct((rows, width), jnp.float32),
             jax.ShapeDtypeStruct((rows,), jnp.float32),
         ),
-        in_specs=[VMEM] * 8,
+        in_specs=[VMEM] * (7 + len(pieces)),
         out_specs=(HBM, HBM, HBM),
         scratch_shapes=[
             pltpu.VMEM((rows, width), jnp.float32),
@@ -284,7 +261,7 @@
         ],
         compiler_params=PARAMS,
         name="finish",
-    )(hit, own, other, turned, mine, request_base, passage_base, everything)
+    )(hit, own, other, *prepared, *pieces)
 
 
 def weigh(request_similarity, passage_similarity, positive, hard_ids, batch_size):

time: 21.2 us -> 21.1 us (level)
  transfers between devices with their start and end apart: 7 -> 7, of which waited for: 5 -> 5; matrix products, arithmetic and copies ran while one was open for 0% -> 0% of each run, Pallas kernels for 1% -> 2%
where the time goes in v4:
time: 21.1 us; the launch traced here: 21 us
  starting transfers between devices  9.86 us (47%)
  waiting for transfers between devices  7.49 us (35%)
  Pallas kernels  2.91 us (14%)
  between operations  0.67 us (3%)
    ppermute x6, starting transfers between devices, exchange(): lax.ppermute(value, 'row', [(i, i ^ mask) for i in range(lax.axis_size('r...  9.79 us
    ppermute x6, waiting for transfers between devices, exchange(): lax.ppermute(value, 'row', [(i, i ^ mask) for i in range(lax.axis_size('r...  6.62 us
    pallas_call x1, Pallas kernels, on_device_fast(): pl.pallas_call(functools.partial(finish_kernel, places, width, PIECES), o...  1.27 us
    pallas_call x1, Pallas kernels, on_device_fast(): pl.pallas_call(pack_kernel, out_shape=(jax.ShapeDtypeStruct((height, widt...  1.02 us
    ppermute x1, waiting for transfers between devices, on_device_fast(): other = lax.ppermute(own, 'col', [(0, 1), (1, 0)])  0.87 us
  transfers between devices with their start and end apart: 7, of which 5 were waited for; matrix products, arithmetic and copies ran while one was open for 0% of the time, Pallas kernels for 2%

profile of v4, /device:TPU:0, one launch (start us, length us, event | category | flops | bytes accessed | tf_op | source)
XLA Modules:
  0.0 21.0 jit_solution(12276261369628739168)
XLA Ops:
  0.6 1.0 %pack.1 = (bf16[16,2176]{1,0:T(8,128)(2,1)S(1)}, f32[8,8]{1,0:T(8,128)S(1)}) custom-call(s32[8]{0:T(128)} %positive_hbm.1, f32[8,2048]{1,0:T(8,128)} %query_hbm.1, f32[8,2048]{1,0:T(8,128)} %doc_hbm.1, s32[8,7]{1,0:T(8,128)} %hard_hbm.1), custom_call_target="tpu_custom_call" | custom-call | tf_op jit(solution)/shard_map/pack/pallas_call | solution.py:199
  1.7 4.1 %collective-permute-start = (bf16[1,16,2176]{2,1,0:T(8,128)(2,1)S(1)}, bf16[1,16,2176]{2,1,0:T(8,128)(2,1)S(1)}, u32[]{:S(2)}, u32[]{:S(2)}) collective-permute-start(bf16[1,16,2176]{2,1,0:T(8,128)(2,1)S(1)} %bitcast.1), channel_id=1, source_target_pairs={{0,8},{2,10},{4,12},{6,14},{8,0},{10,2},{12,4},{14,6},{1,9},{3,11}... | collective-permute-start | bytes 208904 | tf_op jit(solution)/shard_map/ppermute | solution.py:187
  5.8 3.8 %collective-permute-done.refs_1_.refs_8_ = bf16[1,16,2176]{2,1,0:T(8,128)(2,1)S(1)} collective-permute-done((bf16[1,16,2176]{2,1,0:T(8,128)(2,1)S(1)}, bf16[1,16,2176]{2,1,0:T(8,128)(2,1)S(1)}, u32[]{:S(2)}, u32[]{:S(2)}) %collective-permute-start) | collective-permute-done | bytes 69664 | tf_op jit(solution)/shard_map/ppermute | solution.py:187
  9.6 1.6 %collective-permute-start.3 = (bf16[2,16,2176]{2,1,0:T(8,128)(2,1)S(1)}, bf16[2,16,2176]{2,1,0:T(8,128)(2,1)S(1)}, u32[]{:S(2)}, u32[]{:S(2)}) collective-permute-start(bf16[2,16,2176]{2,1,0:T(8,128)(2,1)S(1)} %pad_maximum_fusion), channel_id=1, source_target_pairs={{0,6},{2,4},{4,2},{6,0},{8,14},{10,12},{12,10},{14,8},{1,7},{3,5},... | collective-permute-start | bytes 417800 | tf_op jit(solution)/shard_map/ppermute | solution.py:187
  11.2 0.5 %collective-permute-start.2 = (bf16[1,16,2176]{2,1,0:T(8,128)(2,1)S(1)}, bf16[1,16,2176]{2,1,0:T(8,128)(2,1)S(1)}, u32[]{:S(2)}, u32[]{:S(2)}) collective-permute-start(bf16[1,16,2176]{2,1,0:T(8,128)(2,1)S(1)} %bitcast.3), channel_id=1, source_target_pairs={{0,2},{2,0},{4,6},{6,4},{8,10},{10,8},{12,14},{14,12},{1,3},{3,1},... | collective-permute-start | bytes 208904 | tf_op jit(solution)/shard_map/ppermute | solution.py:187
  11.7 1.4 %collective-permute-start.1 = (bf16[1,16,2176]{2,1,0:T(8,128)(2,1)S(1)}, bf16[1,16,2176]{2,1,0:T(8,128)(2,1)S(1)}, u32[]{:S(2)}, u32[]{:S(2)}) collective-permute-start(bf16[1,16,2176]{2,1,0:T(8,128)(2,1)S(1)} %bitcast.4), channel_id=1, source_target_pairs={{0,4},{2,6},{4,0},{6,2},{8,12},{10,14},{12,8},{14,10},{1,5},{3,7},... | collective-permute-start | bytes 208904 | tf_op jit(solution)/shard_map/ppermute | solution.py:187
  13.1 0.6 %collective-permute-start.5 = (bf16[1,16,2176]{2,1,0:T(8,128)(2,1)S(1)}, bf16[1,16,2176]{2,1,0:T(8,128)(2,1)S(1)}, u32[]{:S(2)}, u32[]{:S(2)}) collective-permute-start(bf16[1,16,2176]{2,1,0:T(8,128)(2,1)S(1)} %collective-permute-done.refs_1_.refs_8_), channel_id=1, source_target_pairs={{0,4},{2,6},{4,0},{6,2},{8,12},{10,14},{12,8},{14,10},{1,5},{3,7},... | collective-permute-start | bytes 208904 | tf_op jit(solution)/shard_map/ppermute | solution.py:187
  13.8 1.5 %collective-permute-start.4 = (bf16[1,16,2176]{2,1,0:T(8,128)(2,1)S(1)}, bf16[1,16,2176]{2,1,0:T(8,128)(2,1)S(1)}, u32[]{:S(2)}, u32[]{:S(2)}) collective-permute-start(bf16[1,16,2176]{2,1,0:T(8,128)(2,1)S(1)} %collective-permute-done.refs_1_.refs_8_), channel_id=1, source_target_pairs={{0,2},{2,0},{4,6},{6,4},{8,10},{10,8},{12,14},{14,12},{1,3},{3,1},... | collective-permute-start | bytes 208904 | tf_op jit(solution)/shard_map/ppermute | solution.py:187
  15.3 2.1 %collective-permute-done.2.refs_3_.refs_10_ = bf16[1,16,2176]{2,1,0:T(8,128)(2,1)S(1)} collective-permute-done((bf16[1,16,2176]{2,1,0:T(8,128)(2,1)S(1)}, bf16[1,16,2176]{2,1,0:T(8,128)(2,1)S(1)}, u32[]{:S(2)}, u32[]{:S(2)}) %collective-permute-start.2) | collective-permute-done | bytes 69664 | tf_op jit(solution)/shard_map/ppermute | solution.py:187
  17.3 0.0 collective-permute-done.1.refs_2_.refs_9_
  17.3 0.6 %collective-permute-done.5.refs_6_.refs_13_ = bf16[1,16,2176]{2,1,0:T(8,128)(2,1)S(1)} collective-permute-done((bf16[1,16,2176]{2,1,0:T(8,128)(2,1)S(1)}, bf16[1,16,2176]{2,1,0:T(8,128)(2,1)S(1)}, u32[]{:S(2)}, u32[]{:S(2)}) %collective-permute-start.5) | collective-permute-done | bytes 69664 | tf_op jit(solution)/shard_map/ppermute | solution.py:187
  17.9 0.2 %collective-permute-done.4.refs_5_.refs_12_ = bf16[1,16,2176]{2,1,0:T(8,128)(2,1)S(1)} collective-permute-done((bf16[1,16,2176]{2,1,0:T(8,128)(2,1)S(1)}, bf16[1,16,2176]{2,1,0:T(8,128)(2,1)S(1)}, u32[]{:S(2)}, u32[]{:S(2)}) %collective-permute-start.4) | collective-permute-done | bytes 69664 | tf_op jit(solution)/shard_map/ppermute | solution.py:187
  18.1 0.0 collective-permute-done.3.refs_4_.refs_11_
  18.1 0.3 %score.1.refs_1_ = f32[72,128]{1,0:T(8,128)S(1)} custom-call(bf16[1,16,2176]{2,1,0:T(8,128)(2,1)S(1)} %bitcast.5, bf16[1,16,2176]{2,1,0:T(8,128)(2,1)S(1)} %collective-permute-done.refs_1_.refs_8_, bf16[1,16,2176]{2,1,0:T(8,128)(2,1)S(1)} %collective-permute-done.1.refs_2_.refs_9_, bf16[1,16,2176]{2,1,0:T(8,128)(2,1)S(1)} %collective-permute-done.2.refs_3_.refs_10_, ...), custom_call_target="tpu_custom_call" | custom-call | tf_op jit(solution)/shard_map/score/pallas_call | solution.py:225
  18.4 0.1 collective-permute-start.6
  18.5 0.3 %bias.1 = (f32[64,128]{1,0:T(8,128)S(1)}, f32[16,128]{1,0:T(8,128)S(1)}, f32[8,2048]{1,0:T(8,128)S(1)}, f32[8,2048]{1,0:T(8,128)S(1)}) custom-call(f32[8,8]{1,0:T(8,128)S(1)} %get-tuple-element.9.hit_ref.refs_0_, bf16[1,16,2176]{2,1,0:T(8,128)(2,1)S(1)} %bitcast.6, bf16[1,16,2176]{2,1,0:T(8,128)(2,1)S(1)} %collective-permute-done.refs_1_.refs_8_, ...), custom_call_target="tpu_custom_call" | custom-call | tf_op jit(solution)/shard_map/bias/pallas_call | solution.py:234
  18.8 0.9 %collective-permute-done.6.refs_2_ = f32[72,128]{1,0:T(8,128)S(1)} collective-permute-done((f32[72,128]{1,0:T(8,128)S(1)}, f32[72,128]{1,0:T(8,128)S(1)}, u32[]{:S(2)}, u32[]{:S(2)}) %collective-permute-start.6) | collective-permute-done | bytes 36896 | tf_op jit(solution)/shard_map/ppermute | solution.py:233
  19.7 1.3 %finish.1 = (f32[8,2048]{1,0:T(8,128)}, f32[8,2048]{1,0:T(8,128)}, f32[8]{0:T(128)}) custom-call(f32[8,8]{1,0:T(8,128)S(1)} %get-tuple-element.9.hit_ref.refs_0_, f32[72,128]{1,0:T(8,128)S(1)} %score.1.refs_1_, f32[72,128]{1,0:T(8,128)S(1)} %collective-permute-done.6.refs_2_, f32[64,128]{1,0:T(8,128)S(1)} %get-tuple-element.11.refs_3_, ...), custom_call_target="tpu_custom_call" | custom-call | tf_op jit(solution)/shard_map/finish/pallas_call | solution.py:247
  (1 shorter events, 0.0 us)
Async XLA Ops:
  1.7 7.9 %collective-permute-start = (bf16[1,16,2176]{2,1,0:T(8,128)(2,1)S(1)}, bf16[1,16,2176]{2,1,0:T(8,128)(2,1)S(1)}, u32[]{:S(2)}, u32[]{:S(2)}) collective-permute-start(bf16[1,16,2176]{2,1,0:T(8,128)(2,1)S(1)} %bitcast.1), channel_id=1, source_target_pairs={{0,8},{2,10},{4,12},{6,14},{8,0},{10,2},{12,4},{14,6},{1,9},{3,11}... | collective-permute-start | bytes 208904 | tf_op jit(solution)/shard_map/ppermute | solution.py:187
  9.6 8.5 %collective-permute-start.3 = (bf16[2,16,2176]{2,1,0:T(8,128)(2,1)S(1)}, bf16[2,16,2176]{2,1,0:T(8,128)(2,1)S(1)}, u32[]{:S(2)}, u32[]{:S(2)}) collective-permute-start(bf16[2,16,2176]{2,1,0:T(8,128)(2,1)S(1)} %pad_maximum_fusion), channel_id=1, source_target_pairs={{0,6},{2,4},{4,2},{6,0},{8,14},{10,12},{12,10},{14,8},{1,7},{3,5},... | collective-permute-start | bytes 417800 | tf_op jit(solution)/shard_map/ppermute | solution.py:187
  11.2 6.1 %collective-permute-start.2 = (bf16[1,16,2176]{2,1,0:T(8,128)(2,1)S(1)}, bf16[1,16,2176]{2,1,0:T(8,128)(2,1)S(1)}, u32[]{:S(2)}, u32[]{:S(2)}) collective-permute-start(bf16[1,16,2176]{2,1,0:T(8,128)(2,1)S(1)} %bitcast.3), channel_id=1, source_target_pairs={{0,2},{2,0},{4,6},{6,4},{8,10},{10,8},{12,14},{14,12},{1,3},{3,1},... | collective-permute-start | bytes 208904 | tf_op jit(solution)/shard_map/ppermute | solution.py:187
  11.7 5.6 %collective-permute-start.1 = (bf16[1,16,2176]{2,1,0:T(8,128)(2,1)S(1)}, bf16[1,16,2176]{2,1,0:T(8,128)(2,1)S(1)}, u32[]{:S(2)}, u32[]{:S(2)}) collective-permute-start(bf16[1,16,2176]{2,1,0:T(8,128)(2,1)S(1)} %bitcast.4), channel_id=1, source_target_pairs={{0,4},{2,6},{4,0},{6,2},{8,12},{10,14},{12,8},{14,10},{1,5},{3,7},... | collective-permute-start | bytes 208904 | tf_op jit(solution)/shard_map/ppermute | solution.py:187
  13.1 4.7 %collective-permute-start.5 = (bf16[1,16,2176]{2,1,0:T(8,128)(2,1)S(1)}, bf16[1,16,2176]{2,1,0:T(8,128)(2,1)S(1)}, u32[]{:S(2)}, u32[]{:S(2)}) collective-permute-start(bf16[1,16,2176]{2,1,0:T(8,128)(2,1)S(1)} %collective-permute-done.refs_1_.refs_8_), channel_id=1, source_target_pairs={{0,4},{2,6},{4,0},{6,2},{8,12},{10,14},{12,8},{14,10},{1,5},{3,7},... | collective-permute-start | bytes 208904 | tf_op jit(solution)/shard_map/ppermute | solution.py:187
  13.8 4.3 %collective-permute-start.4 = (bf16[1,16,2176]{2,1,0:T(8,128)(2,1)S(1)}, bf16[1,16,2176]{2,1,0:T(8,128)(2,1)S(1)}, u32[]{:S(2)}, u32[]{:S(2)}) collective-permute-start(bf16[1,16,2176]{2,1,0:T(8,128)(2,1)S(1)} %collective-permute-done.refs_1_.refs_8_), channel_id=1, source_target_pairs={{0,2},{2,0},{4,6},{6,4},{8,10},{10,8},{12,14},{14,12},{1,3},{3,1},... | collective-permute-start | bytes 208904 | tf_op jit(solution)/shard_map/ppermute | solution.py:187
  18.4 1.3 %collective-permute-start.6 = (f32[72,128]{1,0:T(8,128)S(1)}, f32[72,128]{1,0:T(8,128)S(1)}, u32[]{:S(2)}, u32[]{:S(2)}) collective-permute-start(f32[72,128]{1,0:T(8,128)S(1)} %score.1.refs_1_), channel_id=1, source_target_pairs={{0,1},{1,0},{2,3},{3,2},{4,5},{5,4},{6,7},{7,6},{8,9},{9,8},{10,11... | collective-permute-start | bytes 110600 | tf_op jit(solution)/shard_map/ppermute | solution.py:233

commit v5 on v4

--- a/solution.py
+++ b/solution.py
@@ -41,25 +41,31 @@
     hard_ref,
     sems,
 ):
+    rows, width = query_ref.shape
+    tail = out_ref.shape[1] - width
+    step = width // READS
+    spans = [pl.ds(n * step, step) for n in range(READS)]
+    pairs = [(positive_hbm, positive_ref), (hard_hbm, hard_ref)]
+    for span in spans:
+        pairs.append((query_hbm.at[:, span], query_ref.at[:, span]))
+        pairs.append((doc_hbm.at[:, span], doc_ref.at[:, span]))
     copies = [
-        pltpu.make_async_copy(source, target, sems.at[n])
-        for n, (source, target) in enumerate(
-            (
-                (positive_hbm, positive_ref),
-                (query_hbm, query_ref),
-                (doc_hbm, doc_ref),
-                (hard_hbm, hard_ref),
-            )
-        )
+        pltpu.make_async_copy(source, target, sems.at[n]) for n, (source, target) in enumerate(pairs)
     ]
     for copy in copies:
         copy.start()
-    for copy in copies:
-        copy.wait()
-    rows, width = query_ref.shape
-    tail = out_ref.shape[1] - width
+    copies[0].wait()
+    copies[1].wait()
     hit = slot_matrix(positive_ref, rows)
     hit_ref[...] = hit
+    chosen = [hit[:, i][:, None] > 0.0 for i in range(rows)]
+
+    def in_slots(value):
+        placed = jnp.zeros_like(value)
+        for i in range(rows):
+            placed = jnp.where(chosen[i], value[i][None, :], placed)
+        return placed
+
     lane = lax.broadcasted_iota(jnp.int32, (rows, tail), 1)
     block, place = lane // (2 * rows), lax.rem(lane, 2 * rows)
     column = jnp.where(place >= rows, block * rows + place - rows, -1)
@@ -67,19 +73,30 @@
     counts = jnp.zeros((rows, tail), jnp.float32)
     for k in range(hard.shape[1]):
         counts = counts + jnp.where(hard[:, k][:, None] == column, 1.0, 0.0)
-    raw = jnp.concatenate([query_ref[...], counts], axis=1)
-    upper = jnp.zeros_like(raw)
-    for i in range(rows):
-        upper = jnp.where(hit[:, i][:, None] > 0.0, raw[i][None, :], upper)
-    lower = jnp.concatenate([doc_ref[...], jnp.zeros((rows, tail), jnp.float32)], axis=1)
-    out_ref[...] = jnp.concatenate([upper, lower], axis=0).astype(jnp.bfloat16)
+    out_ref[:, width:] = jnp.concatenate(
+        [in_slots(counts), jnp.zeros_like(counts)], axis=0
+    ).astype(jnp.bfloat16)
+    for n, span in enumerate(spans):
+        copies[2 + 2 * n].wait()
+        copies[3 + 2 * n].wait()
+        out_ref[:, span] = jnp.concatenate(
+            [in_slots(query_ref[:, span]), doc_ref[:, span]], axis=0
+        ).astype(jnp.bfloat16)
 
 
 def stack(refs, places, start, stop):
     return jnp.concatenate([refs[p][n, :, start:stop] for p, n in places], axis=0)
 
 
-def score_kernel(places, width, *refs):
+def in_order(hit, value):
+    back = hit.T
+    placed = jnp.zeros_like(value)
+    for p in range(value.shape[0]):
+        placed = jnp.where(back[:, p][:, None] > 0.0, value[p][None, :], placed)
+    return placed
+
+
+def score_kernel(places, width, hit_ref, *refs):
     *block_refs, score_ref = refs
     values = stack(block_refs, places, 0, width)
     product = lax.dot_general(
@@ -89,11 +106,12 @@
     rows = height // 2
     by_block = product.reshape(blocks, height, blocks * height)
     score_ref[: blocks * rows] = by_block[:, rows:].reshape(blocks * rows, blocks * height)
-    score_ref[blocks * rows :] = product[:rows]
+    score_ref[blocks * rows :] = in_order(hit_ref[...], product[:rows])
 
 
 def bias_kernel(places, width, hit_ref, *refs):
     *block_refs, turned_ref, mine_ref, request_ref, passage_ref = refs
+    hit = hit_ref[...]
     me = lax.axis_index("row")
     height, blocks = block_refs[0].shape[1], len(places)
     rows, total = height // 2, blocks * height
@@ -115,18 +133,26 @@
         jnp.log1p(hardness_multiplier * counts),
         -jnp.inf,
     )
-    mine_ref[...] = bias[:height]
+    mine_ref[:rows] = in_order(hit, bias[:rows])
+    mine_ref[rows:height] = bias[rows:height]
+    mine_ref[height : height + rows] = jnp.concatenate(
+        [hit.T, jnp.zeros((rows, total - rows), jnp.float32)], axis=1
+    )
+    mine_ref[height + rows :] = jnp.concatenate(
+        [jnp.zeros((rows, rows), jnp.float32), hit.T, jnp.zeros((rows, total - height), jnp.float32)],
+        axis=1,
+    )
     turned_ref[...] = bias.T.reshape(blocks, height, total)[:, rows:].reshape(blocks * rows, total)
     block = block_refs[0]
-    back = hit_ref[...].T.astype(jnp.bfloat16)
+    back = hit.T.astype(jnp.bfloat16)
     anchors = jnp.dot(back, block[0, rows:, :width], preferred_element_type=jnp.float32)
     request_ref[...] = anchors * -scale
     passage_ref[...] = block[0, :rows, :width].astype(jnp.float32) * -scale
 
 
 def finish_kernel(places, width, pieces, *refs):
-    hit_ref, own_ref, other_ref, turned_ref, mine_ref, request_base, passage_base = refs[:7]
-    block_refs = refs[7:-7]
+    own_ref, other_ref, turned_ref, mine_ref, request_base, passage_base = refs[:6]
+    block_refs = refs[6:-7]
     request_hbm, passage_hbm, loss_hbm, request_ref, passage_ref, loss_ref, sems = refs[-7:]
     height, blocks = block_refs[0].shape[1], len(places)
     rows, total = height // 2, blocks * height
@@ -146,17 +172,16 @@
     lse = top + jnp.log(mass + partner(mass))
     at = lax.broadcasted_iota(jnp.int32, (rows, total), 1)
     slot = lax.broadcasted_iota(jnp.int32, (rows, total), 0)
-    own_lse = jnp.sum(jnp.where(at == slot, lse, 0.0), axis=1, keepdims=True)
+    slot_lse = jnp.sum(jnp.where(at == slot, lse, 0.0), axis=1, keepdims=True)
+    query_lse = jnp.sum(
+        jnp.where(mine_ref[height : height + rows] > 0.0, lse, 0.0), axis=1, keepdims=True
+    )
     query_logits = scores[documents:] + mine_ref[:rows]
-    query_weights = jnp.exp(query_logits - own_lse)
-    document_weights = jnp.exp(scores[:rows] + mine_ref[rows:] - own_lse)
+    query_weights = jnp.exp(query_logits - query_lse)
+    document_weights = jnp.exp(scores[:rows] + mine_ref[rows:height] - slot_lse)
     onto = jnp.exp(turned[:rows] - lse)
-    back = hit_ref[...].T.astype(jnp.bfloat16)
-    request_weights = jnp.dot(
-        back, query_weights.astype(jnp.bfloat16), preferred_element_type=jnp.float32
-    )
     left = jnp.concatenate(
-        [request_weights, document_weights, onto, jnp.zeros_like(onto)], axis=0
+        [query_weights, document_weights, onto, jnp.zeros_like(onto)], axis=0
     ).astype(jnp.bfloat16)
     copies = []
     step = width // pieces
@@ -175,8 +200,10 @@
                 pltpu.make_async_copy(source.at[:, span], target.at[:, span], sems.at[2 * n + k])
             )
             copies[-1].start()
-    picked = jnp.sum(jnp.where(at == slot + rows, query_logits, 0.0), axis=1, keepdims=True)
-    loss_ref[...] = jnp.sum(hit_ref[...] * (own_lse - picked), axis=0)
+    picked = jnp.sum(
+        jnp.where(mine_ref[height + rows :] > 0.0, query_logits, 0.0), axis=1, keepdims=True
+    )
+    loss_ref[...] = jnp.sum(jnp.where(at == slot, query_lse - picked, 0.0), axis=0)[:rows]
     copies.append(pltpu.make_async_copy(loss_ref, loss_hbm, sems.at[2 * pieces]))
     copies[-1].start()
     for copy in copies:
@@ -188,6 +215,7 @@
 
 
 PIECES = 4
+READS = 2
 PLAN = (((0,), 4), ((0,), 2), ((0,), 1), ((0, 1), 3), ((1,), 1), ((1,), 2))
 
 
@@ -209,7 +237,7 @@
             pltpu.VMEM(queries.shape, queries.dtype),
             pltpu.VMEM(documents.shape, documents.dtype),
             pltpu.VMEM(hard_ids.shape, hard_ids.dtype),
-            pltpu.SemaphoreType.DMA((4,)),
+            pltpu.SemaphoreType.DMA((2 + 2 * READS,)),
         ],
         compiler_params=PARAMS,
         name="pack",
@@ -225,17 +253,17 @@
     own = pl.pallas_call(
         functools.partial(score_kernel, places, width),
         out_shape=jax.ShapeDtypeStruct((total // 2 + rows, total), jnp.float32),
-        in_specs=[VMEM] * len(pieces),
+        in_specs=[VMEM] * (1 + len(pieces)),
         out_specs=VMEM,
         compiler_params=PARAMS,
         name="score",
-    )(*pieces)
+    )(hit, *pieces)
     other = lax.ppermute(own, "col", [(0, 1), (1, 0)])
     prepared = pl.pallas_call(
         functools.partial(bias_kernel, places, width),
         out_shape=(
             jax.ShapeDtypeStruct((total // 2, total), jnp.float32),
-            jax.ShapeDtypeStruct((height, total), jnp.float32),
+            jax.ShapeDtypeStruct((2 * height, total), jnp.float32),
             jax.ShapeDtypeStruct((rows, width), jnp.float32),
             jax.ShapeDtypeStruct((rows, width), jnp.float32),
         ),
@@ -251,7 +279,7 @@
             jax.ShapeDtypeStruct((rows, width), jnp.float32),
             jax.ShapeDtypeStruct((rows,), jnp.float32),
         ),
-        in_specs=[VMEM] * (7 + len(pieces)),
+        in_specs=[VMEM] * (6 + len(pieces)),
         out_specs=(HBM, HBM, HBM),
         scratch_shapes=[
             pltpu.VMEM((rows, width), jnp.float32),
@@ -261,7 +289,7 @@
         ],
         compiler_params=PARAMS,
         name="finish",
-    )(hit, own, other, *prepared, *pieces)
+    )(own, other, *prepared, *pieces)
 
 
 def weigh(request_similarity, passage_similarity, positive, hard_ids, batch_size):

time: 21.1 us -> 20.9 us (level)
  Pallas kernels: 2.91 us -> 2.66 us
where the time goes in v5:
time: 20.9 us; the launch traced here: 20.7 us
  starting transfers between devices  9.86 us (47%)
  waiting for transfers between devices  7.5 us (36%)
  Pallas kernels  2.66 us (13%)
  between operations  0.67 us (3%)
    ppermute x6, starting transfers between devices, exchange(): lax.ppermute(value, 'row', [(i, i ^ mask) for i in range(lax.axis_size('r...  9.79 us
    ppermute x6, waiting for transfers between devices, exchange(): lax.ppermute(value, 'row', [(i, i ^ mask) for i in range(lax.axis_size('r...  6.62 us
    pallas_call x1, Pallas kernels, on_device_fast(): pl.pallas_call(functools.partial(finish_kernel, places, width, PIECES), o...  1.15 us
    pallas_call x1, Pallas kernels, on_device_fast(): pl.pallas_call(pack_kernel, out_shape=(jax.ShapeDtypeStruct((height, widt...  0.89 us
    ppermute x1, waiting for transfers between devices, on_device_fast(): other = lax.ppermute(own, 'col', [(0, 1), (1, 0)])  0.87 us
  transfers between devices with their start and end apart: 7, of which 5 were waited for; matrix products, arithmetic and copies ran while one was open for 0% of the time, Pallas kernels for 2%

profile of v5, /device:TPU:0, one launch (start us, length us, event | category | flops | bytes accessed | tf_op | source)
XLA Modules:
  0.0 20.7 jit_solution(14511551091223277941)
XLA Ops:
  0.6 0.9 %pack.1 = (bf16[16,2176]{1,0:T(8,128)(2,1)S(1)}, f32[8,8]{1,0:T(8,128)S(1)}) custom-call(s32[8]{0:T(128)} %positive_hbm.1, f32[8,2048]{1,0:T(8,128)} %query_hbm.1, f32[8,2048]{1,0:T(8,128)} %doc_hbm.1, s32[8,7]{1,0:T(8,128)} %hard_hbm.1), custom_call_target="tpu_custom_call" | custom-call | tf_op jit(solution)/shard_map/pack/pallas_call | solution.py:227
  1.5 4.1 %collective-permute-start = (bf16[1,16,2176]{2,1,0:T(8,128)(2,1)S(1)}, bf16[1,16,2176]{2,1,0:T(8,128)(2,1)S(1)}, u32[]{:S(2)}, u32[]{:S(2)}) collective-permute-start(bf16[1,16,2176]{2,1,0:T(8,128)(2,1)S(1)} %bitcast.1), channel_id=1, source_target_pairs={{0,8},{2,10},{4,12},{6,14},{8,0},{10,2},{12,4},{14,6},{1,9},{3,11}... | collective-permute-start | bytes 208904 | tf_op jit(solution)/shard_map/ppermute | solution.py:214
  5.7 3.8 %collective-permute-done.refs_1_.refs_7_ = bf16[1,16,2176]{2,1,0:T(8,128)(2,1)S(1)} collective-permute-done((bf16[1,16,2176]{2,1,0:T(8,128)(2,1)S(1)}, bf16[1,16,2176]{2,1,0:T(8,128)(2,1)S(1)}, u32[]{:S(2)}, u32[]{:S(2)}) %collective-permute-start) | collective-permute-done | bytes 69664 | tf_op jit(solution)/shard_map/ppermute | solution.py:214
  9.5 1.6 %collective-permute-start.3 = (bf16[2,16,2176]{2,1,0:T(8,128)(2,1)S(1)}, bf16[2,16,2176]{2,1,0:T(8,128)(2,1)S(1)}, u32[]{:S(2)}, u32[]{:S(2)}) collective-permute-start(bf16[2,16,2176]{2,1,0:T(8,128)(2,1)S(1)} %pad_maximum_fusion), channel_id=1, source_target_pairs={{0,6},{2,4},{4,2},{6,0},{8,14},{10,12},{12,10},{14,8},{1,7},{3,5},... | collective-permute-start | bytes 417800 | tf_op jit(solution)/shard_map/ppermute | solution.py:214
  11.1 0.5 %collective-permute-start.2 = (bf16[1,16,2176]{2,1,0:T(8,128)(2,1)S(1)}, bf16[1,16,2176]{2,1,0:T(8,128)(2,1)S(1)}, u32[]{:S(2)}, u32[]{:S(2)}) collective-permute-start(bf16[1,16,2176]{2,1,0:T(8,128)(2,1)S(1)} %bitcast.3), channel_id=1, source_target_pairs={{0,2},{2,0},{4,6},{6,4},{8,10},{10,8},{12,14},{14,12},{1,3},{3,1},... | collective-permute-start | bytes 208904 | tf_op jit(solution)/shard_map/ppermute | solution.py:214
  11.6 1.4 %collective-permute-start.1 = (bf16[1,16,2176]{2,1,0:T(8,128)(2,1)S(1)}, bf16[1,16,2176]{2,1,0:T(8,128)(2,1)S(1)}, u32[]{:S(2)}, u32[]{:S(2)}) collective-permute-start(bf16[1,16,2176]{2,1,0:T(8,128)(2,1)S(1)} %bitcast.4), channel_id=1, source_target_pairs={{0,4},{2,6},{4,0},{6,2},{8,12},{10,14},{12,8},{14,10},{1,5},{3,7},... | collective-permute-start | bytes 208904 | tf_op jit(solution)/shard_map/ppermute | solution.py:214
  13.0 0.6 %collective-permute-start.5 = (bf16[1,16,2176]{2,1,0:T(8,128)(2,1)S(1)}, bf16[1,16,2176]{2,1,0:T(8,128)(2,1)S(1)}, u32[]{:S(2)}, u32[]{:S(2)}) collective-permute-start(bf16[1,16,2176]{2,1,0:T(8,128)(2,1)S(1)} %collective-permute-done.refs_1_.refs_7_), channel_id=1, source_target_pairs={{0,4},{2,6},{4,0},{6,2},{8,12},{10,14},{12,8},{14,10},{1,5},{3,7},... | collective-permute-start | bytes 208904 | tf_op jit(solution)/shard_map/ppermute | solution.py:214
  13.6 1.5 %collective-permute-start.4 = (bf16[1,16,2176]{2,1,0:T(8,128)(2,1)S(1)}, bf16[1,16,2176]{2,1,0:T(8,128)(2,1)S(1)}, u32[]{:S(2)}, u32[]{:S(2)}) collective-permute-start(bf16[1,16,2176]{2,1,0:T(8,128)(2,1)S(1)} %collective-permute-done.refs_1_.refs_7_), channel_id=1, source_target_pairs={{0,2},{2,0},{4,6},{6,4},{8,10},{10,8},{12,14},{14,12},{1,3},{3,1},... | collective-permute-start | bytes 208904 | tf_op jit(solution)/shard_map/ppermute | solution.py:214
  15.1 2.1 %collective-permute-done.2.refs_3_.refs_9_ = bf16[1,16,2176]{2,1,0:T(8,128)(2,1)S(1)} collective-permute-done((bf16[1,16,2176]{2,1,0:T(8,128)(2,1)S(1)}, bf16[1,16,2176]{2,1,0:T(8,128)(2,1)S(1)}, u32[]{:S(2)}, u32[]{:S(2)}) %collective-permute-start.2) | collective-permute-done | bytes 69664 | tf_op jit(solution)/shard_map/ppermute | solution.py:214
  17.2 0.0 collective-permute-done.1.refs_2_.refs_8_
  17.2 0.6 %collective-permute-done.5.refs_6_.refs_12_ = bf16[1,16,2176]{2,1,0:T(8,128)(2,1)S(1)} collective-permute-done((bf16[1,16,2176]{2,1,0:T(8,128)(2,1)S(1)}, bf16[1,16,2176]{2,1,0:T(8,128)(2,1)S(1)}, u32[]{:S(2)}, u32[]{:S(2)}) %collective-permute-start.5) | collective-permute-done | bytes 69664 | tf_op jit(solution)/shard_map/ppermute | solution.py:214
  17.7 0.2 %collective-permute-done.4.refs_5_.refs_11_ = bf16[1,16,2176]{2,1,0:T(8,128)(2,1)S(1)} collective-permute-done((bf16[1,16,2176]{2,1,0:T(8,128)(2,1)S(1)}, bf16[1,16,2176]{2,1,0:T(8,128)(2,1)S(1)}, u32[]{:S(2)}, u32[]{:S(2)}) %collective-permute-start.4) | collective-permute-done | bytes 69664 | tf_op jit(solution)/shard_map/ppermute | solution.py:214
  18.0 0.0 collective-permute-done.3.refs_4_.refs_10_
  18.0 0.3 %score.1.refs_0_ = f32[72,128]{1,0:T(8,128)S(1)} custom-call(f32[8,8]{1,0:T(8,128)S(1)} %get-tuple-element.9.hit_ref, bf16[1,16,2176]{2,1,0:T(8,128)(2,1)S(1)} %bitcast.5, bf16[1,16,2176]{2,1,0:T(8,128)(2,1)S(1)} %collective-permute-done.refs_1_.refs_7_, bf16[1,16,2176]{2,1,0:T(8,128)(2,1)S(1)} %collective-permute-done.1.refs_2_.refs_8_, ...), custom_call_target="tpu_custom_call" | custom-call | tf_op jit(solution)/shard_map/score/pallas_call | solution.py:253
  18.3 0.1 collective-permute-start.6
  18.3 0.3 %bias.1 = (f32[64,128]{1,0:T(8,128)S(1)}, f32[32,128]{1,0:T(8,128)S(1)}, f32[8,2048]{1,0:T(8,128)S(1)}, f32[8,2048]{1,0:T(8,128)S(1)}) custom-call(f32[8,8]{1,0:T(8,128)S(1)} %get-tuple-element.9.hit_ref, bf16[1,16,2176]{2,1,0:T(8,128)(2,1)S(1)} %bitcast.6, bf16[1,16,2176]{2,1,0:T(8,128)(2,1)S(1)} %collective-permute-done.refs_1_.refs_7_, ...), custom_call_target="tpu_custom_call" | custom-call | tf_op jit(solution)/shard_map/bias/pallas_call | solution.py:262
  18.7 0.9 %collective-permute-done.6.refs_1_ = f32[72,128]{1,0:T(8,128)S(1)} collective-permute-done((f32[72,128]{1,0:T(8,128)S(1)}, f32[72,128]{1,0:T(8,128)S(1)}, u32[]{:S(2)}, u32[]{:S(2)}) %collective-permute-start.6) | collective-permute-done | bytes 36896 | tf_op jit(solution)/shard_map/ppermute | solution.py:261
  19.5 1.2 %finish.1 = (f32[8,2048]{1,0:T(8,128)}, f32[8,2048]{1,0:T(8,128)}, f32[8]{0:T(128)}) custom-call(f32[72,128]{1,0:T(8,128)S(1)} %score.1.refs_0_, f32[72,128]{1,0:T(8,128)S(1)} %collective-permute-done.6.refs_1_, f32[64,128]{1,0:T(8,128)S(1)} %get-tuple-element.11.refs_2_, f32[32,128]{1,0:T(8,128)S(1)} %get-tuple-element.12.refs_3_, ...), custom_call_target="tpu_custom_call" | custom-call | tf_op jit(solution)/shard_map/finish/pallas_call | solution.py:275
  (1 shorter events, 0.0 us)
Async XLA Ops:
  1.5 7.9 %collective-permute-start = (bf16[1,16,2176]{2,1,0:T(8,128)(2,1)S(1)}, bf16[1,16,2176]{2,1,0:T(8,128)(2,1)S(1)}, u32[]{:S(2)}, u32[]{:S(2)}) collective-permute-start(bf16[1,16,2176]{2,1,0:T(8,128)(2,1)S(1)} %bitcast.1), channel_id=1, source_target_pairs={{0,8},{2,10},{4,12},{6,14},{8,0},{10,2},{12,4},{14,6},{1,9},{3,11}... | collective-permute-start | bytes 208904 | tf_op jit(solution)/shard_map/ppermute | solution.py:214
  9.5 8.5 %collective-permute-start.3 = (bf16[2,16,2176]{2,1,0:T(8,128)(2,1)S(1)}, bf16[2,16,2176]{2,1,0:T(8,128)(2,1)S(1)}, u32[]{:S(2)}, u32[]{:S(2)}) collective-permute-start(bf16[2,16,2176]{2,1,0:T(8,128)(2,1)S(1)} %pad_maximum_fusion), channel_id=1, source_target_pairs={{0,6},{2,4},{4,2},{6,0},{8,14},{10,12},{12,10},{14,8},{1,7},{3,5},... | collective-permute-start | bytes 417800 | tf_op jit(solution)/shard_map/ppermute | solution.py:214
  11.1 6.1 %collective-permute-start.2 = (bf16[1,16,2176]{2,1,0:T(8,128)(2,1)S(1)}, bf16[1,16,2176]{2,1,0:T(8,128)(2,1)S(1)}, u32[]{:S(2)}, u32[]{:S(2)}) collective-permute-start(bf16[1,16,2176]{2,1,0:T(8,128)(2,1)S(1)} %bitcast.3), channel_id=1, source_target_pairs={{0,2},{2,0},{4,6},{6,4},{8,10},{10,8},{12,14},{14,12},{1,3},{3,1},... | collective-permute-start | bytes 208904 | tf_op jit(solution)/shard_map/ppermute | solution.py:214
  11.6 5.6 %collective-permute-start.1 = (bf16[1,16,2176]{2,1,0:T(8,128)(2,1)S(1)}, bf16[1,16,2176]{2,1,0:T(8,128)(2,1)S(1)}, u32[]{:S(2)}, u32[]{:S(2)}) collective-permute-start(bf16[1,16,2176]{2,1,0:T(8,128)(2,1)S(1)} %bitcast.4), channel_id=1, source_target_pairs={{0,4},{2,6},{4,0},{6,2},{8,12},{10,14},{12,8},{14,10},{1,5},{3,7},... | collective-permute-start | bytes 208904 | tf_op jit(solution)/shard_map/ppermute | solution.py:214
  13.0 4.7 %collective-permute-start.5 = (bf16[1,16,2176]{2,1,0:T(8,128)(2,1)S(1)}, bf16[1,16,2176]{2,1,0:T(8,128)(2,1)S(1)}, u32[]{:S(2)}, u32[]{:S(2)}) collective-permute-start(bf16[1,16,2176]{2,1,0:T(8,128)(2,1)S(1)} %collective-permute-done.refs_1_.refs_7_), channel_id=1, source_target_pairs={{0,4},{2,6},{4,0},{6,2},{8,12},{10,14},{12,8},{14,10},{1,5},{3,7},... | collective-permute-start | bytes 208904 | tf_op jit(solution)/shard_map/ppermute | solution.py:214
  13.6 4.3 %collective-permute-start.4 = (bf16[1,16,2176]{2,1,0:T(8,128)(2,1)S(1)}, bf16[1,16,2176]{2,1,0:T(8,128)(2,1)S(1)}, u32[]{:S(2)}, u32[]{:S(2)}) collective-permute-start(bf16[1,16,2176]{2,1,0:T(8,128)(2,1)S(1)} %collective-permute-done.refs_1_.refs_7_), channel_id=1, source_target_pairs={{0,2},{2,0},{4,6},{6,4},{8,10},{10,8},{12,14},{14,12},{1,3},{3,1},... | collective-permute-start | bytes 208904 | tf_op jit(solution)/shard_map/ppermute | solution.py:214
  18.3 1.3 %collective-permute-start.6 = (f32[72,128]{1,0:T(8,128)S(1)}, f32[72,128]{1,0:T(8,128)S(1)}, u32[]{:S(2)}, u32[]{:S(2)}) collective-permute-start(f32[72,128]{1,0:T(8,128)S(1)} %score.1.refs_0_), channel_id=1, source_target_pairs={{0,1},{1,0},{2,3},{3,2},{4,5},{5,4},{6,7},{7,6},{8,9},{9,8},{10,11... | collective-permute-start | bytes 110600 | tf_op jit(solution)/shard_map/ppermute | solution.py:261

commit v6 on v5

--- a/solution.py
+++ b/solution.py
@@ -42,7 +42,7 @@
     sems,
 ):
     rows, width = query_ref.shape
-    tail = out_ref.shape[1] - width
+    tail = out_ref.shape[1] - 2 * width
     step = width // READS
     spans = [pl.ds(n * step, step) for n in range(READS)]
     pairs = [(positive_hbm, positive_ref), (hard_hbm, hard_ref)]
@@ -73,19 +73,20 @@
     counts = jnp.zeros((rows, tail), jnp.float32)
     for k in range(hard.shape[1]):
         counts = counts + jnp.where(hard[:, k][:, None] == column, 1.0, 0.0)
-    out_ref[:, width:] = jnp.concatenate(
-        [in_slots(counts), jnp.zeros_like(counts)], axis=0
-    ).astype(jnp.bfloat16)
+    out_ref[:, 2 * width :] = in_slots(counts).astype(jnp.bfloat16)
     for n, span in enumerate(spans):
         copies[2 + 2 * n].wait()
         copies[3 + 2 * n].wait()
-        out_ref[:, span] = jnp.concatenate(
-            [in_slots(query_ref[:, span]), doc_ref[:, span]], axis=0
-        ).astype(jnp.bfloat16)
-
-
-def stack(refs, places, start, stop):
-    return jnp.concatenate([refs[p][n, :, start:stop] for p, n in places], axis=0)
+        out_ref[:, span] = in_slots(query_ref[:, span]).astype(jnp.bfloat16)
+        out_ref[:, pl.ds(width + n * step, step)] = doc_ref[:, span].astype(jnp.bfloat16)
+
+
+def stack(refs, places, width, start, stop):
+    halves = []
+    for p, n in places:
+        halves.append(refs[p][n, :, start:stop])
+        halves.append(refs[p][n, :, width + start : width + stop])
+    return jnp.concatenate(halves, axis=0)
 
 
 def in_order(hit, value):
@@ -98,11 +99,11 @@
 
 def score_kernel(places, width, hit_ref, *refs):
     *block_refs, score_ref = refs
-    values = stack(block_refs, places, 0, width)
+    values = stack(block_refs, places, width, 0, width)
     product = lax.dot_general(
         values, values, (((1,), (1,)), ((), ())), preferred_element_type=jnp.float32
     )
-    height, blocks = block_refs[0].shape[1], len(places)
+    height, blocks = 2 * block_refs[0].shape[1], len(places)
     rows = height // 2
     by_block = product.reshape(blocks, height, blocks * height)
     score_ref[: blocks * rows] = by_block[:, rows:].reshape(blocks * rows, blocks * height)
@@ -113,9 +114,13 @@
     *block_refs, turned_ref, mine_ref, request_ref, passage_ref = refs
     hit = hit_ref[...]
     me = lax.axis_index("row")
-    height, blocks = block_refs[0].shape[1], len(places)
+    height, blocks = 2 * block_refs[0].shape[1], len(places)
     rows, total = height // 2, blocks * height
-    counts = stack(block_refs, places, width, width + total).astype(jnp.float32)
+    counts = []
+    for p, n in places:
+        counts.append(block_refs[p][n, :, 2 * width : 2 * width + total].astype(jnp.float32))
+        counts.append(jnp.zeros_like(counts[-1]))
+    counts = jnp.concatenate(counts, axis=0)
     row = lax.broadcasted_iota(jnp.int32, (total, total), 0)
     lane = lax.broadcasted_iota(jnp.int32, (total, total), 1)
     bit = 1
@@ -145,16 +150,16 @@
     turned_ref[...] = bias.T.reshape(blocks, height, total)[:, rows:].reshape(blocks * rows, total)
     block = block_refs[0]
     back = hit.T.astype(jnp.bfloat16)
-    anchors = jnp.dot(back, block[0, rows:, :width], preferred_element_type=jnp.float32)
+    anchors = jnp.dot(back, block[0, :, width : 2 * width], preferred_element_type=jnp.float32)
     request_ref[...] = anchors * -scale
-    passage_ref[...] = block[0, :rows, :width].astype(jnp.float32) * -scale
+    passage_ref[...] = block[0, :, :width].astype(jnp.float32) * -scale
 
 
 def finish_kernel(places, width, pieces, *refs):
     own_ref, other_ref, turned_ref, mine_ref, request_base, passage_base = refs[:6]
     block_refs = refs[6:-7]
     request_hbm, passage_hbm, loss_hbm, request_ref, passage_ref, loss_ref, sems = refs[-7:]
-    height, blocks = block_refs[0].shape[1], len(places)
+    height, blocks = 2 * block_refs[0].shape[1], len(places)
     rows, total = height // 2, blocks * height
     documents = blocks * rows
     scores = (own_ref[...] + other_ref[...]) * scale
@@ -187,7 +192,7 @@
     step = width // pieces
     for n in range(pieces):
         span = pl.ds(n * step, step)
-        values = stack(block_refs, places, n * step, (n + 1) * step)
+        values = stack(block_refs, places, width, n * step, (n + 1) * step)
         product = jnp.dot(left, values, preferred_element_type=jnp.float32)
         request_ref[:, span] = product[:rows] * scale + request_base[:, span]
         passage_ref[:, span] = (
@@ -216,7 +221,7 @@
 
 PIECES = 4
 READS = 2
-PLAN = (((0,), 4), ((0,), 2), ((0,), 1), ((0, 1), 3), ((1,), 1), ((1,), 2))
+PLAN = (((0,), 4), ((0,), 2), ((0,), 3), ((0, 1), 1), ((1,), 3), ((1,), 2))
 
 
 def on_device_fast(queries, documents, positive, hard_ids):
@@ -227,7 +232,7 @@
     block, hit = pl.pallas_call(
         pack_kernel,
         out_shape=(
-            jax.ShapeDtypeStruct((height, width + tail), jnp.bfloat16),
+            jax.ShapeDtypeStruct((rows, 2 * width + tail), jnp.bfloat16),
             jax.ShapeDtypeStruct((rows, rows), jnp.float32),
         ),
         in_specs=[HBM, HBM, HBM, HBM],

time: 20.9 us -> 22.1 us (1.057)
  starting transfers between devices: 9.86 us -> 10.9 us
    ppermute x6, starting transfers between devices: 9.79 us -> 10.8 us  [exchange(): lax.ppermute(value, 'row', [(i, i ^ mask) for i in range(lax.axis_size('r...]
  transfers between devices with their start and end apart: 7 -> 7, of which waited for: 5 -> 5; matrix products, arithmetic and copies ran while one was open for 0% -> 0% of each run, Pallas kernels for 2% -> 1%
where the time goes in v6:
time: 22.1 us; the launch traced here: 21.9 us
  starting transfers between devices  10.9 us (49%)
  waiting for transfers between devices  7.58 us (34%)
  Pallas kernels  2.68 us (12%)
  between operations  0.67 us (3%)
    ppermute x6, starting transfers between devices, exchange(): lax.ppermute(value, 'row', [(i, i ^ mask) for i in range(lax.axis_size('r...  10.8 us
    ppermute x6, waiting for transfers between devices, exchange(): lax.ppermute(value, 'row', [(i, i ^ mask) for i in range(lax.axis_size('r...  6.71 us
    pallas_call x1, Pallas kernels, on_device_fast(): pl.pallas_call(functools.partial(finish_kernel, places, width, PIECES), o...  1.16 us
    pallas_call x1, Pallas kernels, on_device_fast(): pl.pallas_call(pack_kernel, out_shape=(jax.ShapeDtypeStruct((rows, 2 * wi...  0.89 us
    ppermute x1, waiting for transfers between devices, on_device_fast(): other = lax.ppermute(own, 'col', [(0, 1), (1, 0)])  0.87 us
  transfers between devices with their start and end apart: 7, of which 5 were waited for; matrix products, arithmetic and copies ran while one was open for 0% of the time, Pallas kernels for 1%

profile of v6, /device:TPU:0, one launch (start us, length us, event | category | flops | bytes accessed | tf_op | source)
XLA Modules:
  0.0 21.9 jit_solution(3494437622389553394)
XLA Ops:
  0.6 0.9 %pack.1 = (bf16[8,4224]{1,0:T(8,128)(2,1)S(1)}, f32[8,8]{1,0:T(8,128)S(1)}) custom-call(s32[8]{0:T(128)} %positive_hbm.1, f32[8,2048]{1,0:T(8,128)} %query_hbm.1, f32[8,2048]{1,0:T(8,128)} %doc_hbm.1, s32[8,7]{1,0:T(8,128)} %hard_hbm.1), custom_call_target="tpu_custom_call" | custom-call | tf_op jit(solution)/shard_map/pack/pallas_call | solution.py:232
  1.5 4.1 %collective-permute-start = (bf16[1,8,4224]{2,1,0:T(8,128)(2,1)S(1)}, bf16[1,8,4224]{2,1,0:T(8,128)(2,1)S(1)}, u32[]{:S(2)}, u32[]{:S(2)}) collective-permute-start(bf16[1,8,4224]{2,1,0:T(8,128)(2,1)S(1)} %bitcast.1), channel_id=1, source_target_pairs={{0,8},{2,10},{4,12},{6,14},{8,0},{10,2},{12,4},{14,6},{1,9},{3,11}... | collective-permute-start | bytes 202760 | tf_op jit(solution)/shard_map/ppermute | solution.py:219
  5.7 3.7 %collective-permute-done.refs_1_.refs_7_ = bf16[1,8,4224]{2,1,0:T(8,128)(2,1)S(1)} collective-permute-done((bf16[1,8,4224]{2,1,0:T(8,128)(2,1)S(1)}, bf16[1,8,4224]{2,1,0:T(8,128)(2,1)S(1)}, u32[]{:S(2)}, u32[]{:S(2)}) %collective-permute-start) | collective-permute-done | bytes 67616 | tf_op jit(solution)/shard_map/ppermute | solution.py:219
  9.4 1.8 %collective-permute-start.3 = (bf16[2,8,4224]{2,1,0:T(8,128)(2,1)S(1)}, bf16[2,8,4224]{2,1,0:T(8,128)(2,1)S(1)}, u32[]{:S(2)}, u32[]{:S(2)}) collective-permute-start(bf16[2,8,4224]{2,1,0:T(8,128)(2,1)S(1)} %pad_maximum_fusion), channel_id=1, source_target_pairs={{0,2},{2,0},{4,6},{6,4},{8,10},{10,8},{12,14},{14,12},{1,3},{3,1},... | collective-permute-start | bytes 405512 | tf_op jit(solution)/shard_map/ppermute | solution.py:219
  11.2 0.4 %collective-permute-start.2 = (bf16[1,8,4224]{2,1,0:T(8,128)(2,1)S(1)}, bf16[1,8,4224]{2,1,0:T(8,128)(2,1)S(1)}, u32[]{:S(2)}, u32[]{:S(2)}) collective-permute-start(bf16[1,8,4224]{2,1,0:T(8,128)(2,1)S(1)} %bitcast.3), channel_id=1, source_target_pairs={{0,6},{2,4},{4,2},{6,0},{8,14},{10,12},{12,10},{14,8},{1,7},{3,5},... | collective-permute-start | bytes 202760 | tf_op jit(solution)/shard_map/ppermute | solution.py:219
  11.5 1.4 %collective-permute-start.1 = (bf16[1,8,4224]{2,1,0:T(8,128)(2,1)S(1)}, bf16[1,8,4224]{2,1,0:T(8,128)(2,1)S(1)}, u32[]{:S(2)}, u32[]{:S(2)}) collective-permute-start(bf16[1,8,4224]{2,1,0:T(8,128)(2,1)S(1)} %bitcast.4), channel_id=1, source_target_pairs={{0,4},{2,6},{4,0},{6,2},{8,12},{10,14},{12,8},{14,10},{1,5},{3,7},... | collective-permute-start | bytes 202760 | tf_op jit(solution)/shard_map/ppermute | solution.py:219
  13.0 0.6 %collective-permute-start.5 = (bf16[1,8,4224]{2,1,0:T(8,128)(2,1)S(1)}, bf16[1,8,4224]{2,1,0:T(8,128)(2,1)S(1)}, u32[]{:S(2)}, u32[]{:S(2)}) collective-permute-start(bf16[1,8,4224]{2,1,0:T(8,128)(2,1)S(1)} %collective-permute-done.refs_1_.refs_7_), channel_id=1, source_target_pairs={{0,4},{2,6},{4,0},{6,2},{8,12},{10,14},{12,8},{14,10},{1,5},{3,7},... | collective-permute-start | bytes 202760 | tf_op jit(solution)/shard_map/ppermute | solution.py:219
  13.5 2.6 %collective-permute-start.4 = (bf16[1,8,4224]{2,1,0:T(8,128)(2,1)S(1)}, bf16[1,8,4224]{2,1,0:T(8,128)(2,1)S(1)}, u32[]{:S(2)}, u32[]{:S(2)}) collective-permute-start(bf16[1,8,4224]{2,1,0:T(8,128)(2,1)S(1)} %collective-permute-done.refs_1_.refs_7_), channel_id=1, source_target_pairs={{0,6},{2,4},{4,2},{6,0},{8,14},{10,12},{12,10},{14,8},{1,7},{3,5},... | collective-permute-start | bytes 202760 | tf_op jit(solution)/shard_map/ppermute | solution.py:219
  16.1 0.8 %collective-permute-done.2.refs_3_.refs_9_ = bf16[1,8,4224]{2,1,0:T(8,128)(2,1)S(1)} collective-permute-done((bf16[1,8,4224]{2,1,0:T(8,128)(2,1)S(1)}, bf16[1,8,4224]{2,1,0:T(8,128)(2,1)S(1)}, u32[]{:S(2)}, u32[]{:S(2)}) %collective-permute-start.2) | collective-permute-done | bytes 67616 | tf_op jit(solution)/shard_map/ppermute | solution.py:219
  16.9 0.0 collective-permute-done.1.refs_2_.refs_8_
  16.9 0.5 %collective-permute-done.5.refs_6_.refs_12_ = bf16[1,8,4224]{2,1,0:T(8,128)(2,1)S(1)} collective-permute-done((bf16[1,8,4224]{2,1,0:T(8,128)(2,1)S(1)}, bf16[1,8,4224]{2,1,0:T(8,128)(2,1)S(1)}, u32[]{:S(2)}, u32[]{:S(2)}) %collective-permute-start.5) | collective-permute-done | bytes 67616 | tf_op jit(solution)/shard_map/ppermute | solution.py:219
  17.5 1.7 %collective-permute-done.4.refs_5_.refs_11_ = bf16[1,8,4224]{2,1,0:T(8,128)(2,1)S(1)} collective-permute-done((bf16[1,8,4224]{2,1,0:T(8,128)(2,1)S(1)}, bf16[1,8,4224]{2,1,0:T(8,128)(2,1)S(1)}, u32[]{:S(2)}, u32[]{:S(2)}) %collective-permute-start.4) | collective-permute-done | bytes 67616 | tf_op jit(solution)/shard_map/ppermute | solution.py:219
  19.1 0.0 collective-permute-done.3.refs_4_.refs_10_
  19.1 0.3 %score.1.refs_0_ = f32[72,128]{1,0:T(8,128)S(1)} custom-call(f32[8,8]{1,0:T(8,128)S(1)} %get-tuple-element.9.hit_ref, bf16[1,8,4224]{2,1,0:T(8,128)(2,1)S(1)} %bitcast.5, bf16[1,8,4224]{2,1,0:T(8,128)(2,1)S(1)} %collective-permute-done.refs_1_.refs_7_, bf16[1,8,4224]{2,1,0:T(8,128)(2,1)S(1)} %collective-permute-done.1.refs_2_.refs_8_, ...), custom_call_target="tpu_custom_call" | custom-call | tf_op jit(solution)/shard_map/score/pallas_call | solution.py:258
  19.4 0.1 collective-permute-start.6
  19.5 0.3 %bias.1 = (f32[64,128]{1,0:T(8,128)S(1)}, f32[32,128]{1,0:T(8,128)S(1)}, f32[8,2048]{1,0:T(8,128)S(1)}, f32[8,2048]{1,0:T(8,128)S(1)}) custom-call(f32[8,8]{1,0:T(8,128)S(1)} %get-tuple-element.9.hit_ref, bf16[1,8,4224]{2,1,0:T(8,128)(2,1)S(1)} %bitcast.6, bf16[1,8,4224]{2,1,0:T(8,128)(2,1)S(1)} %collective-permute-done.refs_1_.refs_7_, ...), custom_call_target="tpu_custom_call" | custom-call | tf_op jit(solution)/shard_map/bias/pallas_call | solution.py:267
  19.8 0.9 %collective-permute-done.6.refs_1_ = f32[72,128]{1,0:T(8,128)S(1)} collective-permute-done((f32[72,128]{1,0:T(8,128)S(1)}, f32[72,128]{1,0:T(8,128)S(1)}, u32[]{:S(2)}, u32[]{:S(2)}) %collective-permute-start.6) | collective-permute-done | bytes 36896 | tf_op jit(solution)/shard_map/ppermute | solution.py:266
  20.7 1.2 %finish.1 = (f32[8,2048]{1,0:T(8,128)}, f32[8,2048]{1,0:T(8,128)}, f32[8]{0:T(128)}) custom-call(f32[72,128]{1,0:T(8,128)S(1)} %score.1.refs_0_, f32[72,128]{1,0:T(8,128)S(1)} %collective-permute-done.6.refs_1_, f32[64,128]{1,0:T(8,128)S(1)} %get-tuple-element.11.refs_2_, f32[32,128]{1,0:T(8,128)S(1)} %get-tuple-element.12.refs_3_, ...), custom_call_target="tpu_custom_call" | custom-call | tf_op jit(solution)/shard_map/finish/pallas_call | solution.py:280
  (1 shorter events, 0.0 us)
Async XLA Ops:
  1.5 7.8 %collective-permute-start = (bf16[1,8,4224]{2,1,0:T(8,128)(2,1)S(1)}, bf16[1,8,4224]{2,1,0:T(8,128)(2,1)S(1)}, u32[]{:S(2)}, u32[]{:S(2)}) collective-permute-start(bf16[1,8,4224]{2,1,0:T(8,128)(2,1)S(1)} %bitcast.1), channel_id=1, source_target_pairs={{0,8},{2,10},{4,12},{6,14},{8,0},{10,2},{12,4},{14,6},{1,9},{3,11}... | collective-permute-start | bytes 202760 | tf_op jit(solution)/shard_map/ppermute | solution.py:219
  9.4 9.7 %collective-permute-start.3 = (bf16[2,8,4224]{2,1,0:T(8,128)(2,1)S(1)}, bf16[2,8,4224]{2,1,0:T(8,128)(2,1)S(1)}, u32[]{:S(2)}, u32[]{:S(2)}) collective-permute-start(bf16[2,8,4224]{2,1,0:T(8,128)(2,1)S(1)} %pad_maximum_fusion), channel_id=1, source_target_pairs={{0,2},{2,0},{4,6},{6,4},{8,10},{10,8},{12,14},{14,12},{1,3},{3,1},... | collective-permute-start | bytes 405512 | tf_op jit(solution)/shard_map/ppermute | solution.py:219
  11.2 5.8 %collective-permute-start.2 = (bf16[1,8,4224]{2,1,0:T(8,128)(2,1)S(1)}, bf16[1,8,4224]{2,1,0:T(8,128)(2,1)S(1)}, u32[]{:S(2)}, u32[]{:S(2)}) collective-permute-start(bf16[1,8,4224]{2,1,0:T(8,128)(2,1)S(1)} %bitcast.3), channel_id=1, source_target_pairs={{0,6},{2,4},{4,2},{6,0},{8,14},{10,12},{12,10},{14,8},{1,7},{3,5},... | collective-permute-start | bytes 202760 | tf_op jit(solution)/shard_map/ppermute | solution.py:219
  11.5 5.4 %collective-permute-start.1 = (bf16[1,8,4224]{2,1,0:T(8,128)(2,1)S(1)}, bf16[1,8,4224]{2,1,0:T(8,128)(2,1)S(1)}, u32[]{:S(2)}, u32[]{:S(2)}) collective-permute-start(bf16[1,8,4224]{2,1,0:T(8,128)(2,1)S(1)} %bitcast.4), channel_id=1, source_target_pairs={{0,4},{2,6},{4,0},{6,2},{8,12},{10,14},{12,8},{14,10},{1,5},{3,7},... | collective-permute-start | bytes 202760 | tf_op jit(solution)/shard_map/ppermute | solution.py:219
  13.0 4.5 %collective-permute-start.5 = (bf16[1,8,4224]{2,1,0:T(8,128)(2,1)S(1)}, bf16[1,8,4224]{2,1,0:T(8,128)(2,1)S(1)}, u32[]{:S(2)}, u32[]{:S(2)}) collective-permute-start(bf16[1,8,4224]{2,1,0:T(8,128)(2,1)S(1)} %collective-permute-done.refs_1_.refs_7_), channel_id=1, source_target_pairs={{0,4},{2,6},{4,0},{6,2},{8,12},{10,14},{12,8},{14,10},{1,5},{3,7},... | collective-permute-start | bytes 202760 | tf_op jit(solution)/shard_map/ppermute | solution.py:219
  13.5 5.6 %collective-permute-start.4 = (bf16[1,8,4224]{2,1,0:T(8,128)(2,1)S(1)}, bf16[1,8,4224]{2,1,0:T(8,128)(2,1)S(1)}, u32[]{:S(2)}, u32[]{:S(2)}) collective-permute-start(bf16[1,8,4224]{2,1,0:T(8,128)(2,1)S(1)} %collective-permute-done.refs_1_.refs_7_), channel_id=1, source_target_pairs={{0,6},{2,4},{4,2},{6,0},{8,14},{10,12},{12,10},{14,8},{1,7},{3,5},... | collective-permute-start | bytes 202760 | tf_op jit(solution)/shard_map/ppermute | solution.py:219
  19.4 1.3 %collective-permute-start.6 = (f32[72,128]{1,0:T(8,128)S(1)}, f32[72,128]{1,0:T(8,128)S(1)}, u32[]{:S(2)}, u32[]{:S(2)}) collective-permute-start(f32[72,128]{1,0:T(8,128)S(1)} %score.1.refs_0_), channel_id=1, source_target_pairs={{0,1},{1,0},{2,3},{3,2},{4,5},{5,4},{6,7},{7,6},{8,9},{9,8},{10,11... | collective-permute-start | bytes 110600 | tf_op jit(solution)/shard_map/ppermute | solution.py:266
